TPU v7x, 256 devices: a whole 4x4x8 slice. The times are simulated.
256 devices in a mesh: seq: 64 (over z, y, x_hi), batch: 4 (over x_lo, core).
Axes of the slice: x: 4 (x_hi: 2, x_lo: 2; x = x_hi * 2 + x_lo), y: 4, z: 8, core: 2. Of those that a mesh axis runs over, the one named last changes fastest.
Arguments:
- queries: bfloat16 [131072, 384], P(('batch', 'seq')), parts along dimension 0, may hold values from -400 to 400
- key_states: bfloat16 [131072, 384], P(('batch', 'seq')), parts along dimension 0, may hold values from -6 to 6
- value_states: bfloat16 [131072, 384], P(('batch', 'seq')), parts along dimension 0, may hold values from -6 to 6
- grad_output: bfloat16 [131072, 384], P(('batch', 'seq')), parts along dimension 0, may hold values from -6 to 6
- partners: int32 [12, 64], P('batch'), parts along dimension 0, may hold values from 0 to 63, each once within a row
- global_blocks: int32 [8], P('batch'), parts along dimension 0, may hold values from 0 to 63
Outputs:
- attended: bfloat16 [131072, 384], P(('batch', 'seq')), parts along dimension 0
- grad_queries: bfloat16 [131072, 384], P(('batch', 'seq')), parts along dimension 0
- grad_keys: bfloat16 [131072, 384], P(('batch', 'seq')), parts along dimension 0
- grad_values: bfloat16 [131072, 384], P(('batch', 'seq')), parts along dimension 0
There are 4 independent parts, one for each index of `batch`. A program takes and returns all parts, laid end to end along the dimension named above; each array names one. Nothing has to cross between parts.
Inputs may be any that keep to these rules, and one draw needn't show every extreme that they name: `partners`: each row names every sequence block once.
All inputs are finite; a program needn't handle non-finite values.
Results may differ from a plain program's by a relative error of at most 0.0065.
Values may be sent and summed in bfloat16 or wider, within the bound.
A program may use at most 128 MiB of HBM per device.

v0:
```python
import math

import jax
import jax.numpy as jnp
from jax import lax
from jax.sharding import PartitionSpec as P

HEADS = 6
HD = 64


def extended(x, sides, width):
    for axis, dim in sides:
        devices, length = (lax.axis_size(axis), x.shape[dim])
        up = [(i, (i + 1) % devices) for i in range(devices)]
        down = [(j, i) for i, j in up]
        last = lax.slice_in_dim(x, length - width, length, axis=dim)
        first = lax.slice_in_dim(x, 0, width, axis=dim)
        before = lax.ppermute(last, axis, up)
        after = lax.ppermute(first, axis, down)
        x = jnp.concatenate([before, x, after], axis=dim)
    return x


def from_behind(x, axis, by):
    devices = lax.axis_size(axis)
    return lax.ppermute(x, axis, [(i, (i + by) % devices) for i in range(devices)])


def head_split(matrix):
    return matrix.reshape(matrix.shape[0], HEADS, HD).transpose(1, 0, 2)


def head_join(stacked):
    return stacked.transpose(1, 0, 2).reshape(stacked.shape[1], HEADS * HD)


def attend(queries, key_rows, grad_output):
    features = queries.shape[1]
    scale = 1.0 / math.sqrt(HD)
    contract_last = (((1,), (1,)), ((), ()))
    contract_first = (((0,), (0,)), ((), ()))

    def per_head(head_items):
        query_head, key_head, value_head, grad_head = head_items
        scores = (
            lax.dot_general(query_head, key_head, contract_last, preferred_element_type=jnp.float32)
            * scale
        )
        row_peak = jnp.max(scores, axis=-1, keepdims=True)
        exponent = jnp.exp(scores - row_peak)
        weights = exponent / jnp.sum(exponent, axis=-1, keepdims=True)
        weights_low = weights.astype(jnp.bfloat16)
        output_head = jnp.dot(weights_low, value_head, preferred_element_type=jnp.float32).astype(
            jnp.bfloat16
        )
        grad_weights = lax.dot_general(
            grad_head, value_head, contract_last, preferred_element_type=jnp.float32
        )
        row_dots = jnp.sum(weights * grad_weights, axis=-1, keepdims=True)
        grad_scores = (weights * (grad_weights - row_dots) * scale).astype(jnp.bfloat16)
        grad_query = jnp.dot(grad_scores, key_head, preferred_element_type=jnp.float32).astype(
            jnp.bfloat16
        )
        grad_key = lax.dot_general(
            grad_scores, query_head, contract_first, preferred_element_type=jnp.float32
        )
        grad_value = lax.dot_general(
            weights_low, grad_head, contract_first, preferred_element_type=jnp.float32
        )
        return (output_head, grad_query, grad_key, grad_value)

    outputs, grad_query, grad_key, grad_value = lax.map(
        per_head,
        (
            head_split(queries),
            head_split(key_rows[:, :features]),
            head_split(key_rows[:, features:]),
            head_split(grad_output),
        ),
    )
    grad_pair = jnp.concatenate([head_join(grad_key), head_join(grad_value)], axis=1)
    return (head_join(outputs), head_join(grad_query), grad_pair)


def route_forward(key_value, route_table, devices):
    block_rows, columns = key_value.shape
    pieces = key_value.reshape(devices, block_rows // devices, columns)
    spread = lax.all_to_all(pieces, "seq", split_axis=0, concat_axis=0, tiled=True)
    picked = jnp.take(spread, route_table, axis=0)
    arrived = lax.all_to_all(picked, "seq", split_axis=1, concat_axis=1, tiled=True)
    return arrived.reshape(route_table.shape[0], block_rows, columns)


def route_back(grad_terms, route_table, devices):
    routes, block_rows, columns = grad_terms.shape
    piece_rows = block_rows // devices
    pieces = grad_terms.reshape(routes, devices, piece_rows, columns)
    coming = lax.all_to_all(pieces, "seq", split_axis=1, concat_axis=1, tiled=True)
    block_ids = jnp.arange(devices, dtype=jnp.int32)
    one_hot = (route_table[:, :, None] == block_ids[None, None, :]).astype(jnp.float32)
    summed = jnp.einsum(
        "rds,rdx->sx",
        one_hot,
        coming.reshape(routes, devices, piece_rows * columns),
        precision=lax.Precision.HIGHEST,
    )
    returned = lax.all_to_all(
        summed.reshape(devices, piece_rows, columns), "seq", split_axis=0, concat_axis=0, tiled=True
    )
    return returned.reshape(block_rows, columns)


def local(queries, key_states, value_states, grad_output, partners, global_blocks):
    devices = lax.axis_size("seq")
    block_rows = queries.shape[0]
    features = queries.shape[1]
    key_value = jnp.concatenate([key_states, value_states], axis=1)
    table_rows = []
    table_rows = table_rows + [partners[0], partners[1], partners[2]]
    table_rows = table_rows + [
        jnp.full((devices,), global_blocks[0], jnp.int32),
        jnp.full((devices,), global_blocks[1], jnp.int32),
    ]
    route_table = jnp.stack(table_rows)
    fetched = route_forward(key_value, route_table, devices)
    padded = extended(key_value, (("seq", 0),), block_rows)
    left_block = padded[:block_rows]
    right_block = padded[2 * block_rows :]
    offset = 0
    random_blocks = [fetched[offset], fetched[offset + 1], fetched[offset + 2]]
    global_rows = [fetched[offset + 3], fetched[offset + 4]]
    key_rows = jnp.concatenate(
        [key_value, left_block, right_block] + random_blocks + global_rows, axis=0
    )
    attended, grad_queries, grad_pair = attend(queries, key_rows, grad_output)
    grad_parts = grad_pair.reshape(8, block_rows, 2 * features)
    grad_total = grad_parts[0]
    returning = []
    grad_total = grad_total + from_behind(grad_parts[1], "seq", -1)
    grad_total = grad_total + from_behind(grad_parts[2], "seq", 1)
    returning = returning + [grad_parts[3], grad_parts[4], grad_parts[5]]
    returning = returning + [grad_parts[6], grad_parts[7]]
    grad_total = grad_total + route_back(jnp.stack(returning), route_table, devices)
    return (
        attended,
        grad_queries,
        grad_total[:, :features].astype(jnp.bfloat16),
        grad_total[:, features:].astype(jnp.bfloat16),
    )


def solution(mesh):
    in_specs = (
        P(("batch", "seq"), None),
        P(("batch", "seq"), None),
        P(("batch", "seq"), None),
        P(("batch", "seq"), None),
        P("batch", None),
        P("batch"),
    )
    out_specs = (
        P(("batch", "seq"), None),
        P(("batch", "seq"), None),
        P(("batch", "seq"), None),
        P(("batch", "seq"), None),
    )
    return jax.shard_map(local, mesh=mesh, in_specs=in_specs, out_specs=out_specs, check_vma=False)
```

profile of v0, /device:TPU:28, one launch (start us, length us, event | category | flops | bytes accessed | tf_op | source)
XLA Modules:
  0.0 737.1 jit_solution(6998005378849463226)
XLA Ops:
  4.7 14.3 %all-to-all-start = ((bf16[64,8,768]{2,1,0:T(8,128)(2,1)}), bf16[64,8,768]{2,1,0:T(8,128)(2,1)S(1)}, u32[]{:S(2)}, u32[]{:S(2)}) async-start(bf16[64,8,768]{2,1,0:T(8,128)(2,1)} %bitcast.12), calls=%async_computation | async-start | bytes 1572864 | tf_op jit(solution)/shard_map/all_to_all | solution.py:89
  23.3 18.0 %all-to-all-done = bf16[64,8,768]{2,1,0:T(8,128)(2,1)S(1)} async-done(((bf16[64,8,768]{2,1,0:T(8,128)(2,1)}), bf16[64,8,768]{2,1,0:T(8,128)(2,1)S(1)}, u32[]{:S(2)}, u32[]{:S(2)}) %all-to-all-start) | async-done | bytes 786464 | tf_op jit(solution)/shard_map/all_to_all | solution.py:89
  41.3 3.5 gather_fusion
  49.6 8.6 %all-to-all-start.1 = ((bf16[5,64,8,768]{3,2,0,1:T(8,128)(2,1)}), bf16[5,64,8,768]{3,2,0,1:T(8,128)(2,1)}, u32[]{:S(2)}, u32[]{:S(2)}) async-start(bf16[5,64,8,768]{3,2,0,1:T(8,128)(2,1)} %copy.79), calls=%async_computation.1 | async-start | bytes 7864320 | tf_op jit(solution)/shard_map/all_to_all | solution.py:91
  63.0 95.1 %collective-permute-done = bf16[512,768]{1,0:T(8,128)(2,1)S(1)} collective-permute-done((bf16[512,768]{1,0:T(8,128)(2,1)}, bf16[512,768]{1,0:T(8,128)(2,1)S(1)}, u32[]{:S(2)}, u32[]{:S(2)}) %collective-permute-start) | collective-permute-done | bytes 786464 | tf_op jit(solution)/shard_map/ppermute | solution.py:19
  171.3 6.1 fusion.68
  177.4 3.2 copy.85
  180.6 4.8 copy.86
  185.3 204.0 %while.16 = (s32[]{:T(128)}, bf16[6,512,64]{1,2,0:T(8,128)(2,1)}, bf16[6,512,64]{1,2,0:T(8,128)(2,1)}, f32[6,4096,64]{1,2,0:T(8,128)}, f32[6,4096,64]{1,2,0:T(8,...) while((s32[]{:T(128)}, bf16[6,512,64]{1,2,0:T(8,128)(2,1)}, ...), condition=%wide.region_4.5_spmd, body=%wide.region_0.4_spmd.sunk | while | flops 1644231168 | bytes 143020256 | solution.py:73
  188.4 9.2 %multiply_reduce_fusion.5 = (f32[512]{0:T(512)S(1)}, f32[512,4096]{1,0:T(8,128)}, f32[512,4096]{1,0:T(8,128)}) fusion(f32[512]{0:T(512)S(1)} %fusion.94, f32[512]{0:T(512)S(1)} %get-tuple-element.211, f32[512,4096]{1,0:T(8,128)S(1)} %get-tuple-element.210, bf16[6,4096,64]{1,2,0:T(8,128)(2,1)} %get-tuple-element.242, s32[]{:T(128)} %get-tuple-element.225, ...), kind=kOutput, calls=%fused_computation.2.clone.1 | convolution fusion | flops 278920704 | bytes 25762816 | tf_op jit(solution)/shard_map/while/body/eval_jaxpr/dot_general | solution.py:57
  197.7 8.0 %multiply_convert_fusion.2 = bf16[512,4096]{1,0:T(8,128)(2,1)S(1)} fusion(f32[512,4096]{1,0:T(8,128)} %get-tuple-element.212, f32[512,4096]{1,0:T(8,128)} %get-tuple-element.213, f32[512]{0:T(512)S(1)} %get-tuple-element.214), kind=kLoop, calls=%fused_computation.1.clone.1 | loop fusion | flops 8388608 | bytes 20973568 | tf_op jit(solution)/shard_map/while/body/eval_jaxpr/convert_element_type | solution.py:61
  207.6 5.4 fusion.98
  216.1 3.2 fusion.95
  222.4 9.2 %multiply_reduce_fusion.5 = (f32[512]{0:T(512)S(1)}, f32[512,4096]{1,0:T(8,128)}, f32[512,4096]{1,0:T(8,128)}) fusion(f32[512]{0:T(512)S(1)} %fusion.94, f32[512]{0:T(512)S(1)} %get-tuple-element.211, f32[512,4096]{1,0:T(8,128)S(1)} %get-tuple-element.210, bf16[6,4096,64]{1,2,0:T(8,128)(2,1)} %get-tuple-element.242, s32[]{:T(128)} %get-tuple-element.225, ...), kind=kOutput, calls=%fused_computation.2.clone.1 | convolution fusion | flops 278920704 | bytes 25762816 | tf_op jit(solution)/shard_map/while/body/eval_jaxpr/dot_general | solution.py:57
  231.7 8.0 %multiply_convert_fusion.2 = bf16[512,4096]{1,0:T(8,128)(2,1)S(1)} fusion(f32[512,4096]{1,0:T(8,128)} %get-tuple-element.212, f32[512,4096]{1,0:T(8,128)} %get-tuple-element.213, f32[512]{0:T(512)S(1)} %get-tuple-element.214), kind=kLoop, calls=%fused_computation.1.clone.1 | loop fusion | flops 8388608 | bytes 20973568 | tf_op jit(solution)/shard_map/while/body/eval_jaxpr/convert_element_type | solution.py:61
  241.5 5.5 fusion.98
  247.0 3.1 fusion.96
  250.1 3.2 fusion.95
  256.4 9.2 %multiply_reduce_fusion.5 = (f32[512]{0:T(512)S(1)}, f32[512,4096]{1,0:T(8,128)}, f32[512,4096]{1,0:T(8,128)}) fusion(f32[512]{0:T(512)S(1)} %fusion.94, f32[512]{0:T(512)S(1)} %get-tuple-element.211, f32[512,4096]{1,0:T(8,128)S(1)} %get-tuple-element.210, bf16[6,4096,64]{1,2,0:T(8,128)(2,1)} %get-tuple-element.242, s32[]{:T(128)} %get-tuple-element.225, ...), kind=kOutput, calls=%fused_computation.2.clone.1 | convolution fusion | flops 278920704 | bytes 25762816 | tf_op jit(solution)/shard_map/while/body/eval_jaxpr/dot_general | solution.py:57
  265.7 8.0 %multiply_convert_fusion.2 = bf16[512,4096]{1,0:T(8,128)(2,1)S(1)} fusion(f32[512,4096]{1,0:T(8,128)} %get-tuple-element.212, f32[512,4096]{1,0:T(8,128)} %get-tuple-element.213, f32[512]{0:T(512)S(1)} %get-tuple-element.214), kind=kLoop, calls=%fused_computation.1.clone.1 | loop fusion | flops 8388608 | bytes 20973568 | tf_op jit(solution)/shard_map/while/body/eval_jaxpr/convert_element_type | solution.py:61
  275.6 5.5 fusion.98
  284.2 3.2 fusion.95
  290.5 9.2 %multiply_reduce_fusion.5 = (f32[512]{0:T(512)S(1)}, f32[512,4096]{1,0:T(8,128)}, f32[512,4096]{1,0:T(8,128)}) fusion(f32[512]{0:T(512)S(1)} %fusion.94, f32[512]{0:T(512)S(1)} %get-tuple-element.211, f32[512,4096]{1,0:T(8,128)S(1)} %get-tuple-element.210, bf16[6,4096,64]{1,2,0:T(8,128)(2,1)} %get-tuple-element.242, s32[]{:T(128)} %get-tuple-element.225, ...), kind=kOutput, calls=%fused_computation.2.clone.1 | convolution fusion | flops 278920704 | bytes 25762816 | tf_op jit(solution)/shard_map/while/body/eval_jaxpr/dot_general | solution.py:57
  299.7 8.0 %multiply_convert_fusion.2 = bf16[512,4096]{1,0:T(8,128)(2,1)S(1)} fusion(f32[512,4096]{1,0:T(8,128)} %get-tuple-element.212, f32[512,4096]{1,0:T(8,128)} %get-tuple-element.213, f32[512]{0:T(512)S(1)} %get-tuple-element.214), kind=kLoop, calls=%fused_computation.1.clone.1 | loop fusion | flops 8388608 | bytes 20973568 | tf_op jit(solution)/shard_map/while/body/eval_jaxpr/convert_element_type | solution.py:61
  309.6 5.4 fusion.98
  315.0 3.1 fusion.96
  318.1 3.2 fusion.95
  324.5 9.2 %multiply_reduce_fusion.5 = (f32[512]{0:T(512)S(1)}, f32[512,4096]{1,0:T(8,128)}, f32[512,4096]{1,0:T(8,128)}) fusion(f32[512]{0:T(512)S(1)} %fusion.94, f32[512]{0:T(512)S(1)} %get-tuple-element.211, f32[512,4096]{1,0:T(8,128)S(1)} %get-tuple-element.210, bf16[6,4096,64]{1,2,0:T(8,128)(2,1)} %get-tuple-element.242, s32[]{:T(128)} %get-tuple-element.225, ...), kind=kOutput, calls=%fused_computation.2.clone.1 | convolution fusion | flops 278920704 | bytes 25762816 | tf_op jit(solution)/shard_map/while/body/eval_jaxpr/dot_general | solution.py:57
  333.7 8.0 %multiply_convert_fusion.2 = bf16[512,4096]{1,0:T(8,128)(2,1)S(1)} fusion(f32[512,4096]{1,0:T(8,128)} %get-tuple-element.212, f32[512,4096]{1,0:T(8,128)} %get-tuple-element.213, f32[512]{0:T(512)S(1)} %get-tuple-element.214), kind=kLoop, calls=%fused_computation.1.clone.1 | loop fusion | flops 8388608 | bytes 20973568 | tf_op jit(solution)/shard_map/while/body/eval_jaxpr/convert_element_type | solution.py:61
  343.6 5.4 fusion.98
  349.0 3.1 fusion.96
  352.1 3.2 fusion.95
  358.4 9.2 %multiply_reduce_fusion.5 = (f32[512]{0:T(512)S(1)}, f32[512,4096]{1,0:T(8,128)}, f32[512,4096]{1,0:T(8,128)}) fusion(f32[512]{0:T(512)S(1)} %fusion.94, f32[512]{0:T(512)S(1)} %get-tuple-element.211, f32[512,4096]{1,0:T(8,128)S(1)} %get-tuple-element.210, bf16[6,4096,64]{1,2,0:T(8,128)(2,1)} %get-tuple-element.242, s32[]{:T(128)} %get-tuple-element.225, ...), kind=kOutput, calls=%fused_computation.2.clone.1 | convolution fusion | flops 278920704 | bytes 25762816 | tf_op jit(solution)/shard_map/while/body/eval_jaxpr/dot_general | solution.py:57
  367.7 8.0 %multiply_convert_fusion.2 = bf16[512,4096]{1,0:T(8,128)(2,1)S(1)} fusion(f32[512,4096]{1,0:T(8,128)} %get-tuple-element.212, f32[512,4096]{1,0:T(8,128)} %get-tuple-element.213, f32[512]{0:T(512)S(1)} %get-tuple-element.214), kind=kLoop, calls=%fused_computation.1.clone.1 | loop fusion | flops 8388608 | bytes 20973568 | tf_op jit(solution)/shard_map/while/body/eval_jaxpr/convert_element_type | solution.py:61
  377.6 5.4 fusion.98
  386.1 3.2 fusion.95
  389.3 7.7 %fusion.50 = (f32[512,768]{0,1:T(8,128)}, f32[512,768]{0,1:T(8,128)}, f32[512,768]{0,1:T(8,128)}, f32[512,768]{0,1:T(8,128)}, f32[512,768]{0,1:T(8,128)}, /*index=5*/f32[512,768]{0,1:T(8,128)S(1)}, f32[512,768]{0,1:T(8,128)S(1)}) fusion(f32[4096,384]{0,1:T(8,128)} %bitcast.172, f32[4096,384]{0,1:T(8,128)} %bitcast.174), kind=kLoop, calls=%fused_computation.67 | loop fusion | flops 2752512 | bytes 23592960 | tf_op jit(solution)/shard_map/concatenate | solution.py:82
  419.0 6.9 copy.97
  425.9 12.8 %all-to-all-start.2 = ((f32[5,64,8,768]{3,2,0,1:T(8,128)}), f32[5,64,8,768]{3,2,0,1:T(8,128)}, u32[]{:S(2)}, u32[]{:S(2)}) async-start(f32[5,64,8,768]{3,2,0,1:T(8,128)} %copy.97), calls=%async_computation.2 | async-start | bytes 15728640 | tf_op jit(solution)/shard_map/all_to_all | solution.py:99
  438.8 173.1 %all-to-all-done.2 = f32[5,64,8,768]{3,2,0,1:T(8,128)} async-done(((f32[5,64,8,768]{3,2,0,1:T(8,128)}), f32[5,64,8,768]{3,2,0,1:T(8,128)}, u32[]{:S(2)}, u32[]{:S(2)}) %all-to-all-start.2) | async-done | bytes 7864352 | tf_op jit(solution)/shard_map/all_to_all | solution.py:99
  611.9 7.1 copy.98
  619.0 9.0 %reshape.185 = f32[5,64,6144]{2,1,0:T(8,128)} reshape(f32[5,64,8,768]{3,2,1,0:T(8,128)} %copy.98) | data formatting | bytes 15728640 | tf_op jit(solution)/shard_map/reshape | solution.py:105
  628.0 6.8 fusion.56
  636.9 8.1 %all-to-all-start.3 = ((f32[64,8,768]{2,1,0:T(8,128)}), f32[64,8,768]{2,1,0:T(8,128)S(1)}, u32[]{:S(2)}, u32[]{:S(2)}) async-start(f32[64,8,768]{2,1,0:T(8,128)} %copy.100), calls=%async_computation.3 | async-start | bytes 3145728 | tf_op jit(solution)/shard_map/all_to_all | solution.py:108
  645.6 6.0 collective-permute-start.3
  654.4 28.6 %all-to-all-done.3 = f32[64,8,768]{2,1,0:T(8,128)S(1)} async-done(((f32[64,8,768]{2,1,0:T(8,128)}), f32[64,8,768]{2,1,0:T(8,128)S(1)}, u32[]{:S(2)}, u32[]{:S(2)}) %all-to-all-start.3) | async-done | bytes 1572896 | tf_op jit(solution)/shard_map/all_to_all | solution.py:108
  683.5 43.5 %collective-permute-done.2 = f32[512,768]{0,1:T(8,128)} collective-permute-done((f32[512,768]{0,1:T(8,128)}, f32[512,768]{0,1:T(8,128)}, u32[]{:S(2)}, u32[]{:S(2)}) %collective-permute-start.2) | collective-permute-done | bytes 1572896 | tf_op jit(solution)/shard_map/ppermute | solution.py:27
  727.0 5.2 collective-permute-done.3
  (141 shorter events, 102.9 us)
Async XLA Ops:
  4.7 36.6 %all-to-all-start = ((bf16[64,8,768]{2,1,0:T(8,128)(2,1)}), bf16[64,8,768]{2,1,0:T(8,128)(2,1)S(1)}, u32[]{:S(2)}, u32[]{:S(2)}) async-start(bf16[64,8,768]{2,1,0:T(8,128)(2,1)} %bitcast.12), calls=%async_computation | async-start | bytes 1572864 | tf_op jit(solution)/shard_map/all_to_all | solution.py:89
  21.0 26.3 %copy-start.7 = (s32[5]{0:T(128)}, s32[5]{0:T(128)S(1)}, u32[]{:S(2)}) copy-start(s32[5]{0:T(128)S(1)} %pad.6.clone) | copy-start | bytes 64
  21.7 25.6 %copy-start.9 = (s32[5]{0:T(128)}, s32[5]{0:T(128)S(1)}, u32[]{:S(2)}) copy-start(s32[5]{0:T(128)S(1)} %pad.7.clone) | copy-start | bytes 64
  47.4 14.5 %copy-start.3 = (bf16[512,384]{1,0:T(8,128)(2,1)S(1)}, bf16[512,384]{1,0:T(8,128)(2,1)}, u32[]{:S(2)}) copy-start(bf16[512,384]{1,0:T(8,128)(2,1)} %param.11) | copy-start | bytes 1179652
  49.6 13.2 %copy-start.4 = (bf16[512,384]{1,0:T(8,128)(2,1)S(1)}, bf16[512,384]{1,0:T(8,128)(2,1)}, u32[]{:S(2)}) copy-start(bf16[512,384]{1,0:T(8,128)(2,1)} %param.8) | copy-start | bytes 1179652
  49.6 111.3 %all-to-all-start.1 = ((bf16[5,64,8,768]{3,2,0,1:T(8,128)(2,1)}), bf16[5,64,8,768]{3,2,0,1:T(8,128)(2,1)}, u32[]{:S(2)}, u32[]{:S(2)}) async-start(bf16[5,64,8,768]{3,2,0,1:T(8,128)(2,1)} %copy.79), calls=%async_computation.1 | async-start | bytes 7864320 | tf_op jit(solution)/shard_map/all_to_all | solution.py:91
  58.2 99.9 %collective-permute-start = (bf16[512,768]{1,0:T(8,128)(2,1)}, bf16[512,768]{1,0:T(8,128)(2,1)S(1)}, u32[]{:S(2)}, u32[]{:S(2)}) collective-permute-start(bf16[512,768]{1,0:T(8,128)(2,1)} %get-tuple-element.144), channel_id=1, source_target_pairs={{0,4},{4,8},{8,12},{12,16},{16,20},{20,24},{24,28},{28,32},{32,36}... | collective-permute-start | bytes 2359304 | tf_op jit(solution)/shard_map/ppermute | solution.py:19
  59.8 100.2 %collective-permute-start.1 = (bf16[512,768]{1,0:T(8,128)(2,1)}, bf16[512,768]{1,0:T(8,128)(2,1)S(1)}, u32[]{:S(2)}, u32[]{:S(2)}) collective-permute-start(bf16[512,768]{1,0:T(8,128)(2,1)} %get-tuple-element.144), channel_id=1, source_target_pairs={{4,0},{8,4},{12,8},{16,12},{20,16},{24,20},{28,24},{32,28},{36,32}... | collective-permute-start | bytes 2359304 | tf_op jit(solution)/shard_map/ppermute | solution.py:20
  185.3 1.6 copy-start
  205.7 10.3 %slice-start = ((s8[8388608]{0:T(1024)(128)(4,1)}), s8[4194304]{0:T(1024)(128)(4,1)S(1)}, s32[]{:S(2)}) async-start(s8[8388608]{0:T(1024)(128)(4,1)} %bitcast.169), calls=%async_computation.4 | async-start | bytes 8388608 | tf_op jit(solution)/shard_map/while
  207.6 8.5 %slice-start.1 = ((s8[8388608]{0:T(1024)(128)(4,1)}), s8[4194304]{0:T(1024)(128)(4,1)S(1)}, s32[]{:S(2)}) async-start(s8[8388608]{0:T(1024)(128)(4,1)} %bitcast.169), calls=%async_computation.5 | async-start | bytes 8388608 | tf_op jit(solution)/shard_map/while
  216.1 3.2 copy-start.1
  219.3 1.6 copy-start
  239.7 10.4 %slice-start = ((s8[8388608]{0:T(1024)(128)(4,1)}), s8[4194304]{0:T(1024)(128)(4,1)S(1)}, s32[]{:S(2)}) async-start(s8[8388608]{0:T(1024)(128)(4,1)} %bitcast.169), calls=%async_computation.4 | async-start | bytes 8388608 | tf_op jit(solution)/shard_map/while
  241.5 8.6 %slice-start.1 = ((s8[8388608]{0:T(1024)(128)(4,1)}), s8[4194304]{0:T(1024)(128)(4,1)S(1)}, s32[]{:S(2)}) async-start(s8[8388608]{0:T(1024)(128)(4,1)} %bitcast.169), calls=%async_computation.5 | async-start | bytes 8388608 | tf_op jit(solution)/shard_map/while
  250.1 3.2 copy-start.1
  253.3 1.6 copy-start
  273.7 10.4 %slice-start = ((s8[8388608]{0:T(1024)(128)(4,1)}), s8[4194304]{0:T(1024)(128)(4,1)S(1)}, s32[]{:S(2)}) async-start(s8[8388608]{0:T(1024)(128)(4,1)} %bitcast.169), calls=%async_computation.4 | async-start | bytes 8388608 | tf_op jit(solution)/shard_map/while
  275.6 8.6 %slice-start.1 = ((s8[8388608]{0:T(1024)(128)(4,1)}), s8[4194304]{0:T(1024)(128)(4,1)S(1)}, s32[]{:S(2)}) async-start(s8[8388608]{0:T(1024)(128)(4,1)} %bitcast.169), calls=%async_computation.5 | async-start | bytes 8388608 | tf_op jit(solution)/shard_map/while
  284.2 3.2 copy-start.1
  287.4 1.6 copy-start
  307.8 10.3 %slice-start = ((s8[8388608]{0:T(1024)(128)(4,1)}), s8[4194304]{0:T(1024)(128)(4,1)S(1)}, s32[]{:S(2)}) async-start(s8[8388608]{0:T(1024)(128)(4,1)} %bitcast.169), calls=%async_computation.4 | async-start | bytes 8388608 | tf_op jit(solution)/shard_map/while
  309.6 8.5 %slice-start.1 = ((s8[8388608]{0:T(1024)(128)(4,1)}), s8[4194304]{0:T(1024)(128)(4,1)S(1)}, s32[]{:S(2)}) async-start(s8[8388608]{0:T(1024)(128)(4,1)} %bitcast.169), calls=%async_computation.5 | async-start | bytes 8388608 | tf_op jit(solution)/shard_map/while
  318.1 3.2 copy-start.1
  321.4 1.6 copy-start
  341.8 10.3 %slice-start = ((s8[8388608]{0:T(1024)(128)(4,1)}), s8[4194304]{0:T(1024)(128)(4,1)S(1)}, s32[]{:S(2)}) async-start(s8[8388608]{0:T(1024)(128)(4,1)} %bitcast.169), calls=%async_computation.4 | async-start | bytes 8388608 | tf_op jit(solution)/shard_map/while
  343.6 8.5 %slice-start.1 = ((s8[8388608]{0:T(1024)(128)(4,1)}), s8[4194304]{0:T(1024)(128)(4,1)S(1)}, s32[]{:S(2)}) async-start(s8[8388608]{0:T(1024)(128)(4,1)} %bitcast.169), calls=%async_computation.5 | async-start | bytes 8388608 | tf_op jit(solution)/shard_map/while
  352.1 3.2 copy-start.1
  355.3 1.6 copy-start
  375.7 10.3 %slice-start = ((s8[8388608]{0:T(1024)(128)(4,1)}), s8[4194304]{0:T(1024)(128)(4,1)S(1)}, s32[]{:S(2)}) async-start(s8[8388608]{0:T(1024)(128)(4,1)} %bitcast.169), calls=%async_computation.4 | async-start | bytes 8388608 | tf_op jit(solution)/shard_map/while
  377.6 8.5 %slice-start.1 = ((s8[8388608]{0:T(1024)(128)(4,1)}), s8[4194304]{0:T(1024)(128)(4,1)S(1)}, s32[]{:S(2)}) async-start(s8[8388608]{0:T(1024)(128)(4,1)} %bitcast.169), calls=%async_computation.5 | async-start | bytes 8388608 | tf_op jit(solution)/shard_map/while
  386.0 3.2 copy-start.1
  411.0 5.5 copy-start.2
  425.9 12.8 %copy-start.6 = (s32[3,64]{1,0:T(4,128)S(1)}, s32[3,64]{1,0:T(4,128)}, u32[]{:S(2)}) copy-start(s32[3,64]{1,0:T(4,128)} %param.12) | copy-start | bytes 2308
  425.9 12.8 %copy-start.8 = (s32[5]{0:T(128)S(1)}, s32[5]{0:T(128)}, u32[]{:S(2)}) copy-start(s32[5]{0:T(128)} %copy-done.7) | copy-start | bytes 64
  425.9 12.8 %copy-start.10 = (s32[5]{0:T(128)S(1)}, s32[5]{0:T(128)}, u32[]{:S(2)}) copy-start(s32[5]{0:T(128)} %copy-done.9) | copy-start | bytes 64
  425.9 186.0 %all-to-all-start.2 = ((f32[5,64,8,768]{3,2,0,1:T(8,128)}), f32[5,64,8,768]{3,2,0,1:T(8,128)}, u32[]{:S(2)}, u32[]{:S(2)}) async-start(f32[5,64,8,768]{3,2,0,1:T(8,128)} %copy.97), calls=%async_computation.2 | async-start | bytes 15728640 | tf_op jit(solution)/shard_map/all_to_all | solution.py:99
  628.0 25.5 %copy-start.5 = (bf16[6,512,64]{1,2,0:T(8,128)(2,1)S(1)}, bf16[6,512,64]{1,2,0:T(8,128)(2,1)}, u32[]{:S(2)}) copy-start(bf16[6,512,64]{1,2,0:T(8,128)(2,1)} %get-tuple-element.55) | copy-start | bytes 1179652
  636.9 46.2 %all-to-all-start.3 = ((f32[64,8,768]{2,1,0:T(8,128)}), f32[64,8,768]{2,1,0:T(8,128)S(1)}, u32[]{:S(2)}, u32[]{:S(2)}) async-start(f32[64,8,768]{2,1,0:T(8,128)} %copy.100), calls=%async_computation.3 | async-start | bytes 3145728 | tf_op jit(solution)/shard_map/all_to_all | solution.py:108
  645.0 82.0 %collective-permute-start.2 = (f32[512,768]{0,1:T(8,128)}, f32[512,768]{0,1:T(8,128)}, u32[]{:S(2)}, u32[]{:S(2)}) collective-permute-start(f32[512,768]{0,1:T(8,128)} %get-tuple-element.133), channel_id=1, source_target_pairs={{0,252},{4,0},{8,4},{12,8},{16,12},{20,16},{24,20},{28,24},{32,28}... | collective-permute-start | bytes 4718600 | tf_op jit(solution)/shard_map/ppermute | solution.py:27
  645.6 86.6 %collective-permute-start.3 = (f32[512,768]{0,1:T(8,128)}, f32[512,768]{0,1:T(8,128)}, u32[]{:S(2)}, u32[]{:S(2)}) collective-permute-start(f32[512,768]{0,1:T(8,128)} %get-tuple-element.134), channel_id=1, source_target_pairs={{0,4},{4,8},{8,12},{12,16},{16,20},{20,24},{24,28},{28,32},{32,36}... | collective-permute-start | bytes 4718600 | tf_op jit(solution)/shard_map/ppermute | solution.py:27
where the time goes:
time: 739 us; the launch traced here: 737 us
  waiting for transfers between devices  364 us (49%)
  matrix products  152 us (21%)
  local copies, waits for them, and re-layouts  93.9 us (13%)
  other arithmetic  72 us (10%)
  starting transfers between devices  54 us (7%)
    all_to_all x1, waiting for transfers between devices, route_back(): lax.all_to_all(pieces, 'seq', split_axis=1, concat_axis=1, tiled=True)  173 us
    ppermute x1, waiting for transfers between devices, extended(): before = lax.ppermute(last, axis, up)  95.1 us
    dot_general x6, matrix products, per_head(): lax.dot_general(grad_head, value_head, contract_last, preferred_element_t...  55.5 us
    ppermute x2, waiting for transfers between devices, from_behind(): lax.ppermute(x, axis, [(i, (i + by) % devices) for i in range(devices)])  48.7 us
    convert_element_type x6, other arithmetic, per_head(): (weights * (grad_weights - row_dots) * scale).astype(jnp.bfloat16)  48.3 us
    dot_general x6, matrix products, per_head(): lax.dot_general(weights_low, grad_head, contract_first, preferred_element...  32.6 us
    all_to_all x1, waiting for transfers between devices, route_back(): lax.all_to_all(summed.reshape(devices, piece_rows, columns), 'seq', split...  28.6 us
    unnamed x35, local copies, waits for them, and re-layouts  27.6 us
  transfers between devices with their start and end apart: 8, of which 7 were waited for; matrix products, arithmetic and copies ran while one was open for 1% of the time, Pallas kernels for 0%

commit v1 on v0

v1 whole, which is shorter than its diff:
```python
import functools
import math

import jax
import jax.numpy as jnp
from jax import lax
from jax.experimental import pallas as pl
from jax.experimental.pallas import tpu as pltpu
from jax.sharding import PartitionSpec as P

F32 = jnp.float32
BF = jnp.bfloat16
LOG2E = math.log2(math.e)
MESH = pl.DeviceIdType.MESH

PAIRS = 3
BLOCK = 512
SEQ = 64
NZ, NY = 8, 4


def split(device):
    return device // 8, (device // 2) % 4, device % 2


def peers(me, start, stop, body):
    @pl.loop(start, stop)
    def _(k):
        body((me + k) % SEQ)


def remote(src, dst, send, recv, device):
    return pltpu.make_async_remote_copy(
        src_ref=src, dst_ref=dst, send_sem=send, recv_sem=recv, device_id={"seq": device}, device_id_type=MESH
    )


def local(src, dst, sem):
    return pltpu.make_async_copy(src, dst, sem)


def drain(ref, sem):
    pltpu.make_async_copy(ref, ref, sem).wait()


def rows(tiles):
    return tiles.reshape(BLOCK, 128)


def tiles(block):
    return block.reshape(NZ, NY, 16, 128)


def prepare(pair, kv, q_ref, do_ref, kt, vt, qt, qm):
    cols = slice(pair * 128, pair * 128 + 128)
    qs = q_ref[:, cols] * jnp.asarray(0.125, BF)
    lane = lax.broadcasted_iota(jnp.int32, (BLOCK, 128), 1)
    row = lax.broadcasted_iota(jnp.int32, (128, BLOCK), 0)
    qst = qs.T
    for h in range(2):
        qm[h] = jnp.where((lane >= 64) == (h == 1), qs, jnp.zeros_like(qs))
        qt[h] = jnp.where((row >= 64) == (h == 1), qst, jnp.zeros_like(qst))

    @pl.loop(0, 8)
    def _(j):
        kt[j] = rows(kv[pair, 0, j]).T
        t = rows(kv[pair, 1, j]).T
        for h in range(2):
            vt[h, j, 0:64] = t[64 * h : 64 * h + 64]
            vt[h, j, 64:80] = jnp.ones((16, BLOCK), BF)


def head(pair, h, kv, dkv, do_ref, ot, dqt, s_buf, p_buf, kt, vt, qt, qm):
    do_t = do_ref[:, pair * 128 : pair * 128 + 128].astype(F32).T
    qth = qt[h]

    def scores(j, peak):
        s = jnp.dot(rows(kv[pair, 0, j]), qth, preferred_element_type=F32)
        s_buf[j] = s
        return jnp.maximum(peak, jnp.max(s.reshape(BLOCK // 8, 8, BLOCK), axis=0))

    peak = lax.fori_loop(0, 8, scores, jnp.full((8, BLOCK), -jnp.inf, F32))
    peak = jnp.max(peak, axis=0, keepdims=True) * LOG2E

    def weigh(j, acc):
        p = jnp.exp2(s_buf[j] * LOG2E - peak).astype(BF)
        p_buf[j] = p
        return acc + jnp.dot(vt[h, j], p, preferred_element_type=F32)

    acc = lax.fori_loop(0, 8, weigh, jnp.zeros((80, BLOCK), F32))
    inverse = 1.0 / acc[64:65]
    out = acc[0:64] * inverse
    ot[64 * h : 64 * h + 64] = out
    do_n = (do_t[64 * h : 64 * h + 64] * inverse).astype(BF)
    dots = jnp.sum(do_n.astype(F32) * out, axis=0, keepdims=True)
    zero = jnp.zeros((64, BLOCK), BF)
    do_full = jnp.concatenate([do_n, zero] if h == 0 else [zero, do_n], axis=0)
    do_rows = do_full.T
    qmh = qm[h]

    def backward(j, acc):
        p = p_buf[j]
        gw = jnp.dot(rows(kv[pair, 1, j]), do_full, preferred_element_type=F32)
        ds = (p.astype(F32) * (gw - dots)).astype(BF)
        dk = jnp.dot(ds, qmh, preferred_element_type=F32).astype(BF)
        dv = jnp.dot(p, do_rows, preferred_element_type=F32).astype(BF)
        if h == 0:
            dkv[pair, 0, j] = tiles(dk)
            dkv[pair, 1, j] = tiles(dv)
        else:
            dkv[pair, 0, j] = dkv[pair, 0, j] + tiles(dk)
            dkv[pair, 1, j] = dkv[pair, 1, j] + tiles(dv)
        return acc + jnp.dot(kt[j, 64 * h : 64 * h + 64], ds, preferred_element_type=F32)

    dq = lax.fori_loop(0, 8, backward, jnp.zeros((64, BLOCK), F32))
    dqt[64 * h : 64 * h + 64] = dq * 0.125


def kernel(
    table, inverse, hot, q_ref, do_ref, k_ref, v_ref, o_ref, dq_ref, gk_ref, gv_ref,
    kv, dkv, spread, picked, gsel, coming0, coming1, coming2, near, rsy, ysum, rsx, xsum, rsz, ret, retin,
    s_buf, p_buf, kt, vt, qt, qm, ot, dqt,
    load_sem, own_sem, p1_send, p1_recv, p2_send, p2_recv, nb_send, nb_recv,
    gz_send, gz_recv, gx_send, gx_recv, gy_send, gy_recv,
    b1_send, b1_recv, bn_send, bn_recv, ry_send, ry_recv, rx_send, rx_recv, rz_send, rz_recv, b2_send, b2_recv,
):
    coming = (coming0, coming1, coming2)
    me = lax.axis_index("seq")
    z, y, x = split(me)
    right, left = (me + 1) % SEQ, (me + SEQ - 1) % SEQ

    loads = []
    for pair in range(PAIRS):
        for which, ref in enumerate((k_ref, v_ref)):
            loads.append(local(ref.at[:, :, :, pair * 128 : pair * 128 + 128], kv.at[pair, which, 0], load_sem.at[pair, which]))
    for copy in loads:
        copy.start()

    barrier = pltpu.get_barrier_semaphore()

    def hello(device):
        pl.semaphore_signal(barrier, inc=1, device_id={"seq": device}, device_id_type=MESH)

    peers(me, 1, SEQ, hello)
    pl.semaphore_wait(barrier, SEQ - 1)
    for copy in loads:
        copy.wait()

    def scatter(d):
        dz, dy, dx = split(d)
        remote(kv.at[:, dx, 0, dz, dy], spread.at[me], p1_send, p1_recv, d).start()

    own = local(kv.at[:, x, 0, z, y], spread.at[me], own_sem.at[0])
    own.start()
    peers(me, 1, SEQ, scatter)

    def neighbours(pair):
        return [
            remote(kv.at[pair, :, 0], kv.at[pair, :, 1], nb_send.at[pair, 0], nb_recv.at[pair, 0], right),
            remote(kv.at[pair, :, 0], kv.at[pair, :, 2], nb_send.at[pair, 1], nb_recv.at[pair, 1], left),
        ]

    def start_neighbours(pair):
        for copy in neighbours(pair):
            copy.start()

    start_neighbours(0)
    own.wait()
    drain(spread.at[pl.ds(0, SEQ - 1)], p1_recv)

    for g in range(2):
        gsel[:, g] = spread[table[3 + g, 0]]
    own_g = local(gsel, kv.at[:, x, 6:8, z, y], own_sem.at[1])
    own_g.start()

    @pl.loop(1, NZ)
    def _(k):
        d = ((z + k) % NZ) * 8 + y * 2 + x
        remote(gsel, kv.at[:, x, 6:8, z, y], gz_send, gz_recv, d).start()

    def pick(pair):
        @pl.loop(0, SEQ)
        def _(d):
            for r in range(3):
                picked[pair, d, r] = spread[table[r, d], pair]

    def start_routes(pair):
        local(picked.at[pair, me], kv.at[pair, x, 3:6, z, y], own_sem.at[2 + pair]).start()

        def send(d):
            remote(picked.at[pair, d], kv.at[pair, x, 3:6, z, y], p2_send.at[pair], p2_recv.at[pair], d).start()

        peers(me, 1, SEQ, send)

    pick(0)
    start_routes(0)
    own_g.wait()
    drain(kv.at[:, x, 6:8, 0 : NZ - 1, y], gz_recv)
    across = [
        remote(kv.at[pair, x, 6:8, :, y], kv.at[pair, x, 6:8, :, y], gx_send.at[pair], gx_recv.at[pair], z * 8 + y * 2 + 1 - x)
        for pair in range(PAIRS)
    ]
    for copy in across:
        copy.start()
    pick(1)
    pick(2)
    for pair in range(PAIRS):
        across[pair].wait_recv()

        @pl.loop(1, NY)
        def _(k):
            d = z * 8 + ((y + k) % NY) * 2 + x
            remote(kv.at[pair, :, 6:8, :, y], kv.at[pair, :, 6:8, :, y], gy_send.at[pair], gy_recv.at[pair], d).start()

    for pair in range(1, PAIRS):
        start_neighbours(pair)
        start_routes(pair)

    def arrive(pair):
        for copy in neighbours(pair):
            copy.wait_recv()
        local(picked.at[pair, me], kv.at[pair, x, 3:6, z, y], own_sem.at[2 + pair]).wait()
        drain(picked.at[pair, pl.ds(0, SEQ - 1)], p2_recv.at[pair])
        drain(kv.at[pair, :, 6:8, :, 0 : NY - 1], gy_recv.at[pair])

    def back_neighbours(pair):
        return [
            remote(dkv.at[pair, :, 1], near.at[pair, 0], bn_send.at[pair, 0], bn_recv.at[pair, 0], left),
            remote(dkv.at[pair, :, 2], near.at[pair, 1], bn_send.at[pair, 1], bn_recv.at[pair, 1], right),
        ]

    def back_own(pair):
        return local(dkv.at[pair, x, 3:6, z, y], coming[pair].at[me], own_sem.at[5 + pair])

    def stage0(pair):
        for k in range(1, NY):
            to = (y + k) % NY
            remote(
                dkv.at[pair, :, 6:8, :, to], rsy.at[pair, k - 1], ry_send.at[pair, k - 1], ry_recv.at[pair, k - 1],
                z * 8 + to * 2 + x,
            ).start()
        back_own(pair).start()

        def send(d):
            dz, dy, dx = split(d)
            remote(dkv.at[pair, dx, 3:6, dz, dy], coming[pair].at[me], b1_send.at[pair], b1_recv.at[pair], d).start()

        peers(me, 1, SEQ, send)
        for copy in back_neighbours(pair):
            copy.start()

    def stage1_copy(pair):
        return remote(ysum.at[pair, 1 - x], rsx.at[pair], rx_send.at[pair], rx_recv.at[pair], z * 8 + y * 2 + 1 - x)

    def stage1(pair):
        for k in range(1, NY):
            drain(rsy.at[pair, k - 1], ry_recv.at[pair, k - 1])
        for which in range(2):
            total = dkv[pair, which, 6:8, :, y].astype(F32)
            for k in range(NY - 1):
                total = total + rsy[pair, k, which].astype(F32)
            ysum[pair, which] = total.astype(BF)
        stage1_copy(pair).start()

    def stage2(pair):
        stage1_copy(pair).wait_recv()
        xsum[pair] = (ysum[pair, x].astype(F32) + rsx[pair].astype(F32)).astype(BF)
        for k in range(1, NZ):
            to = (z + k) % NZ
            remote(
                xsum.at[pair, :, to], rsz.at[pair, k - 1], rz_send.at[pair, k - 1], rz_recv.at[pair, k - 1],
                to * 8 + y * 2 + x,
            ).start()

    def stage3(pair):
        for k in range(1, NZ):
            drain(rsz.at[pair, k - 1], rz_recv.at[pair, k - 1])
        shared = xsum[pair, :, z].astype(F32)
        for k in range(NZ - 1):
            shared = shared + rsz[pair, k].astype(F32)
        back_own(pair).wait()
        drain(coming[pair].at[pl.ds(0, SEQ - 1)], b1_recv.at[pair])

        @pl.loop(0, SEQ)
        def _(c):
            total = hot[0, c] * shared[0] + hot[1, c] * shared[1]
            for r in range(3):
                total = total + coming[pair][inverse[r, c], r].astype(F32)
            ret[pair, c] = total.astype(BF)

        local(ret.at[pair, me], retin.at[pair, x, z, y], own_sem.at[8 + pair]).start()

        def send(d):
            remote(ret.at[pair, d], retin.at[pair, x, z, y], b2_send.at[pair], b2_recv.at[pair], d).start()

        peers(me, 1, SEQ, send)

    def stage4(pair):
        for copy in back_neighbours(pair):
            copy.wait_recv()
        local(ret.at[pair, me], retin.at[pair, x, z, y], own_sem.at[8 + pair]).wait()
        drain(ret.at[pair, pl.ds(0, SEQ - 1)], b2_recv.at[pair])
        for which, ref in enumerate((gk_ref, gv_ref)):
            total = dkv[pair, which, 0].astype(F32) + retin[pair, which].astype(F32)
            total = total + near[pair, 0, which].astype(F32) + near[pair, 1, which].astype(F32)
            ref[:, pair * 128 : pair * 128 + 128] = rows(total.astype(BF))

    def begin(pair):
        arrive(pair)
        prepare(pair, kv, q_ref, do_ref, kt, vt, qt, qm)

    def half(pair, h):
        head(pair, h, kv, dkv, do_ref, ot, dqt, s_buf, p_buf, kt, vt, qt, qm)

    def finish(pair):
        cols = slice(pair * 128, pair * 128 + 128)
        o_ref[:, cols] = ot[...].T.astype(BF)
        dq_ref[:, cols] = dqt[...].T.astype(BF)

    begin(0)
    half(0, 0)
    half(0, 1)
    stage0(0)
    finish(0)
    begin(1)
    half(1, 0)
    stage1(0)
    half(1, 1)
    stage0(1)
    stage2(0)
    finish(1)
    begin(2)
    half(2, 0)
    stage3(0)
    stage1(1)
    half(2, 1)
    stage0(2)
    stage2(1)
    finish(2)
    stage1(2)
    stage3(1)
    stage2(2)
    stage4(0)
    stage3(2)
    stage4(1)
    stage4(2)

    drain(spread.at[pl.ds(0, SEQ - 1)], p1_send)
    drain(kv.at[:, x, 6:8, 0 : NZ - 1, y], gz_send)
    for pair in range(PAIRS):
        for copy in neighbours(pair) + back_neighbours(pair):
            copy.wait_send()
        drain(picked.at[pair, pl.ds(0, SEQ - 1)], p2_send.at[pair])
        across[pair].wait_send()
        drain(kv.at[pair, :, 6:8, :, 0 : NY - 1], gy_send.at[pair])
        drain(coming[pair].at[pl.ds(0, SEQ - 1)], b1_send.at[pair])
        for k in range(NY - 1):
            drain(rsy.at[pair, k], ry_send.at[pair, k])
        stage1_copy(pair).wait_send()
        for k in range(NZ - 1):
            drain(rsz.at[pair, k], rz_send.at[pair, k])
        drain(ret.at[pair, pl.ds(0, SEQ - 1)], b2_send.at[pair])


def step(queries, key_states, value_states, grad_output, partners, global_blocks):
    ids = jnp.arange(SEQ, dtype=jnp.int32)
    table = jnp.concatenate([partners, jnp.broadcast_to(global_blocks[:, None], (2, SEQ))], axis=0)
    inverse = jnp.sum(jnp.where(partners[:, :, None] == ids[None, None, :], ids[None, :, None], 0), axis=1)
    hot = (global_blocks[:, None] == ids[None, :]).astype(F32)
    vmem = pl.BlockSpec(memory_space=pltpu.VMEM)
    smem = pl.BlockSpec(memory_space=pltpu.SMEM)
    anywhere = pl.BlockSpec(memory_space=pl.ANY)
    scratch = [
        pltpu.VMEM((PAIRS, 2, 8, NZ, NY, 16, 128), BF),
        pltpu.VMEM((PAIRS, 2, 8, NZ, NY, 16, 128), BF),
        pltpu.VMEM((SEQ, PAIRS, 16, 128), BF),
        pltpu.VMEM((PAIRS, SEQ, 3, 16, 128), BF),
        pltpu.VMEM((PAIRS, 2, 16, 128), BF),
        pltpu.VMEM((SEQ, 3, 16, 128), BF),
        pltpu.VMEM((SEQ, 3, 16, 128), BF),
        pltpu.VMEM((SEQ, 3, 16, 128), BF),
        pltpu.VMEM((PAIRS, 2, 2, NZ, NY, 16, 128), BF),
        pltpu.VMEM((PAIRS, NY - 1, 2, 2, NZ, 16, 128), BF),
        pltpu.VMEM((PAIRS, 2, 2, NZ, 16, 128), BF),
        pltpu.VMEM((PAIRS, 2, NZ, 16, 128), BF),
        pltpu.VMEM((PAIRS, 2, NZ, 16, 128), BF),
        pltpu.VMEM((PAIRS, NZ - 1, 2, 16, 128), BF),
        pltpu.VMEM((PAIRS, SEQ, 16, 128), BF),
        pltpu.VMEM((PAIRS, 2, NZ, NY, 16, 128), BF),
        pltpu.VMEM((8, BLOCK, BLOCK), F32),
        pltpu.VMEM((8, BLOCK, BLOCK), BF),
        pltpu.VMEM((8, 128, BLOCK), BF),
        pltpu.VMEM((2, 8, 80, BLOCK), BF),
        pltpu.VMEM((2, 128, BLOCK), BF),
        pltpu.VMEM((2, BLOCK, 128), BF),
        pltpu.VMEM((128, BLOCK), F32),
        pltpu.VMEM((128, BLOCK), F32),
    ]
    dma = pltpu.SemaphoreType.DMA
    sems = [
        dma((PAIRS, 2)), dma((11,)), dma(()), dma(()), dma((PAIRS,)), dma((PAIRS,)), dma((PAIRS, 2)), dma((PAIRS, 2)),
        dma(()), dma(()), dma((PAIRS,)), dma((PAIRS,)), dma((PAIRS,)), dma((PAIRS,)),
        dma((PAIRS,)), dma((PAIRS,)), dma((PAIRS, 2)), dma((PAIRS, 2)),
        dma((PAIRS, NY - 1)), dma((PAIRS, NY - 1)), dma((PAIRS,)), dma((PAIRS,)),
        dma((PAIRS, NZ - 1)), dma((PAIRS, NZ - 1)), dma((PAIRS,)), dma((PAIRS,)),
    ]
    grid_rows = (NZ, NY, 16, PAIRS * 128)
    return pl.pallas_call(
        kernel,
        out_shape=tuple(jax.ShapeDtypeStruct((BLOCK, PAIRS * 128), BF) for _ in range(4)),
        in_specs=[smem, smem, smem, vmem, vmem, anywhere, anywhere],
        out_specs=(vmem,) * 4,
        scratch_shapes=scratch + sems,
        compiler_params=pltpu.CompilerParams(
            collective_id=0, has_side_effects=True, vmem_limit_bytes=60 * 1024 * 1024
        ),
    )(table, inverse, hot, queries, grad_output, key_states.reshape(grid_rows), value_states.reshape(grid_rows))


def solution(mesh):
    spec = P(("batch", "seq"), None)
    return jax.shard_map(
        step,
        mesh=mesh,
        in_specs=(spec, spec, spec, spec, P("batch", None), P("batch")),
        out_specs=(spec,) * 4,
        check_vma=False,
    )
```

time: 739 us -> 229 us (0.31)
  waiting for transfers between devices: 364 us -> 0 us
  Pallas kernels: 0 us -> 220 us
  matrix products: 152 us -> 0 us
  local copies, waits for them, and re-layouts: 93.9 us -> 5.57 us
  other arithmetic: 72 us -> 1.91 us
  starting transfers between devices: 54 us -> 0 us
    pallas_call x0 -> x1, Pallas kernels: none -> 220 us  [step(): pl.pallas_call(kernel, out_shape=tuple((jax.ShapeDtypeStruct((BLOCK, PAIR...]
    all_to_all x4 -> x0, waiting for transfers between devices: 220 us -> none  [the longest x1 173 us: route_back(): lax.all_to_all(pieces, 'seq', split_axis=1, concat_axis=1, tiled=True)]
    dot_general x37 -> x0, matrix products: 152 us -> none  [the longest x6 55.5 us: per_head(): lax.dot_general(grad_head, value_head, contract_last, preferred_element_t...]
    ppermute x4 -> x0, waiting for transfers between devices: 145 us -> none  [the longest x1 95.1 us: extended(): before = lax.ppermute(last, axis, up)]
    convert_element_type x6 -> x1, other arithmetic: 48.3 us -> 0.63 us  [step(): hot = (global_blocks[:, None] == ids[None, :]).astype(F32)]
    all_to_all x4 -> x0, starting transfers between devices: 43.8 us -> none  [the longest x1 14.3 us: route_forward(): lax.all_to_all(pieces, 'seq', split_axis=0, concat_axis=0, tiled=True)]
    slice x10 -> x0, local copies, waits for them, and re-layouts: 26.7 us -> none  [the longest x2 10.8 us: attend(): key_rows[:, features:]]
    unnamed x35 -> x14, local copies, waits for them, and re-layouts: 27.6 us -> 5.51 us
  transfers between devices with their start and end apart: 8 -> 0, of which waited for: 7 -> 0; matrix products, arithmetic and copies ran while one was open for 1% -> 0% of each run, Pallas kernels for 0% -> 0%
where the time goes in v1:
time: 229 us; the launch traced here: 228 us
  Pallas kernels  220 us (96%)
  local copies, waits for them, and re-layouts  5.57 us (2%)
    pallas_call x1, Pallas kernels, step(): pl.pallas_call(kernel, out_shape=tuple((jax.ShapeDtypeStruct((BLOCK, PAIR...  220 us
    unnamed x14, local copies, waits for them, and re-layouts  5.51 us

profile of v1, /device:TPU:28, one launch (start us, length us, event | category | flops | bytes accessed | tf_op | source)
XLA Modules:
  0.0 228.3 jit_solution(14376533905307325479)
XLA Ops:
  0.6 0.0 copy-start.4
  0.6 0.6 copy-done.4
  1.3 0.0 copy-start.3
  1.3 0.6 compare_convert_fusion.hot
  1.9 0.1 broadcast_in_dim.10
  2.0 0.0 copy-done.3
  2.0 0.7 select_reduce_fusion.inverse
  2.7 0.6 pad_add_fusion.table
  3.3 220.1 %shard_map.93 = (bf16[512,384]{1,0:T(8,128)(2,1)}, bf16[512,384]{1,0:T(8,128)(2,1)}, bf16[512,384]{1,0:T(8,128)(2,1)}, bf16[512,384]{1,0:T(8,128)(2,1)}) custom-call(s32[5,64]{1,0:T(8,128)} %pad_add_fusion.table, s32[3,64]{1,0:T(4,128)} %select_reduce_fusion.inverse, f32[2,64]{1,0:T(2,128)} %compare_convert_fusion.hot, bf16[512,384]{1,0:T(8,128)(2,1)} %q_ref.1, ...), custom_call_target="tpu_custom_call" | custom-call | tf_op jit(solution)/shard_map/pallas_call | solution.py:408
  223.4 0.0 copy-start.2
  223.4 1.8 copy.14
  225.3 0.0 copy-done.2
  225.3 0.0 copy-start.1
  225.3 0.7 copy.15
  226.0 0.4 copy-done.1
  226.4 0.0 copy-start
  226.4 0.7 copy.16
  227.2 0.4 copy-done
  227.6 0.7 copy.17
Async XLA Ops:
  0.6 0.7 copy-start.4
  1.3 0.7 copy-start.3
  223.4 1.8 copy-start.2
  225.3 1.1 copy-start.1
  226.4 1.1 copy-start

commit v2 on v1

v2 whole, which is shorter than its diff:
```python
import functools
import math

import jax
import jax.numpy as jnp
from jax import lax
from jax.experimental import pallas as pl
from jax.experimental.pallas import tpu as pltpu
from jax.sharding import PartitionSpec as P

F32 = jnp.float32
BF = jnp.bfloat16
LOG2E = math.log2(math.e)
MESH = pl.DeviceIdType.MESH

PAIRS = 3
BLOCK = 512
SEQ = 64
NZ, NY = 8, 4
EDGES = 16


def split(device):
    return device // 8, (device // 2) % 4, device % 2


def peers(me, start, stop, body):
    @pl.loop(start, stop)
    def _(k):
        body((me + k) % SEQ)


def remote(src, dst, send, recv, device):
    return pltpu.make_async_remote_copy(
        src_ref=src, dst_ref=dst, send_sem=send, recv_sem=recv, device_id={"seq": device}, device_id_type=MESH
    )


def local(src, dst, sem):
    return pltpu.make_async_copy(src, dst, sem)


def drain(ref, sem):
    pltpu.make_async_copy(ref, ref, sem).wait()


def edge_device(e):
    return (8 * (e // 2) + SEQ - 1 + e % 2) % SEQ


def edge_block(e):
    return (8 * (e // 2) + SEQ - e % 2) % SEQ


def rows(tiles):
    return tiles.reshape(BLOCK, 128)


def tiles(block):
    return block.reshape(NZ, NY, 16, 128)


def prepare(pair, kv, q_ref, do_ref, kt, vt, qt, qm):
    cols = slice(pair * 128, pair * 128 + 128)
    qs = q_ref[:, cols] * jnp.asarray(0.125, BF)
    lane = lax.broadcasted_iota(jnp.int32, (BLOCK, 128), 1)
    row = lax.broadcasted_iota(jnp.int32, (128, BLOCK), 0)
    qst = qs.T
    for h in range(2):
        qm[h] = jnp.where((lane >= 64) == (h == 1), qs, jnp.zeros_like(qs))
        qt[h] = jnp.where((row >= 64) == (h == 1), qst, jnp.zeros_like(qst))

    @pl.loop(0, 8)
    def _(j):
        kt[j] = rows(kv[pair, 0, j]).T
        t = rows(kv[pair, 1, j]).T
        for h in range(2):
            vt[h, j, 0:64] = t[64 * h : 64 * h + 64]
            vt[h, j, 64:80] = jnp.ones((16, BLOCK), BF)


def head(pair, h, ticks, kv, dkv, do_ref, ot, dqt, s_buf, p_buf, kt, vt, qt, qm):
    do_t = do_ref[:, pair * 128 : pair * 128 + 128].astype(F32).T
    qth = qt[h]

    def scores(j, peak):
        s = jnp.dot(rows(kv[pair, 0, j]), qth, preferred_element_type=F32)
        s_buf[j] = s
        return jnp.maximum(peak, jnp.max(s.reshape(BLOCK // 8, 8, BLOCK), axis=0))

    peak = lax.fori_loop(0, 8, scores, jnp.full((8, BLOCK), -jnp.inf, F32))
    peak = jnp.max(peak, axis=0, keepdims=True) * LOG2E
    ticks[0]()

    def weigh(j, acc):
        p = jnp.exp2(s_buf[j] * LOG2E - peak).astype(BF)
        p_buf[j] = p
        return acc + jnp.dot(vt[h, j], p, preferred_element_type=F32)

    acc = lax.fori_loop(0, 8, weigh, jnp.zeros((80, BLOCK), F32))
    inverse = 1.0 / acc[64:65]
    out = acc[0:64] * inverse
    ot[64 * h : 64 * h + 64] = out
    do_n = (do_t[64 * h : 64 * h + 64] * inverse).astype(BF)
    dots = jnp.sum(do_n.astype(F32) * out, axis=0, keepdims=True)
    zero = jnp.zeros((64, BLOCK), BF)
    do_full = jnp.concatenate([do_n, zero] if h == 0 else [zero, do_n], axis=0)
    do_rows = do_full.T
    qmh = qm[h]
    ticks[1]()

    def backward(j, acc):
        p = p_buf[j]
        gw = jnp.dot(rows(kv[pair, 1, j]), do_full, preferred_element_type=F32)
        ds = (p.astype(F32) * (gw - dots)).astype(BF)
        dk = jnp.dot(ds, qmh, preferred_element_type=F32).astype(BF)
        dv = jnp.dot(p, do_rows, preferred_element_type=F32).astype(BF)
        if h == 0:
            dkv[pair, 0, j] = tiles(dk)
            dkv[pair, 1, j] = tiles(dv)
        else:
            dkv[pair, 0, j] = dkv[pair, 0, j] + tiles(dk)
            dkv[pair, 1, j] = dkv[pair, 1, j] + tiles(dv)
        return acc + jnp.dot(kt[j, 64 * h : 64 * h + 64], ds, preferred_element_type=F32)

    dq = lax.fori_loop(0, 8, backward, jnp.zeros((64, BLOCK), F32))
    dqt[64 * h : 64 * h + 64] = dq * 0.125


def kernel(
    table, inverse, shared_ids, q_ref, do_ref, k_ref, v_ref, o_ref, dq_ref, gk_ref, gv_ref,
    kv, dkv, spread0, spread1, spread2, picked, gsel, coming0, coming1, coming2, extra0, extra1, extra2, far_in, near_out, near_in,
    rsy, ysum, rsx, xsum, rsz, ret, retin,
    s_buf, p_buf, kt, vt, qt, qm, ot, dqt,
    load_sem, own_sem, p1_send, p1_recv, p2_send, p2_recv, na_send, na_recv, nf_send, nf_recv,
    gz_send, gz_recv, gx_send, gx_recv, gy_send, gy_recv,
    b1_send, b1_recv, bf_send, bf_recv, bn_send, bn_recv,
    pc_send, pc_recv, bc_send, bc_recv,
    ry_send, ry_recv, rx_send, rx_recv, rz_send, rz_recv, b2_send, b2_recv,
):
    spread = (spread0, spread1, spread2)
    coming = (coming0, coming1, coming2)
    extra = (extra0, extra1, extra2)
    me = lax.axis_index("seq")
    z, y, x = split(me)
    twin = z * 8 + y * 2 + 1 - x
    up = (me + 2) % SEQ
    down = (me + SEQ - 2) % SEQ
    ahead = up * (1 - x) + down * x
    behind = down * (1 - x) + up * x
    near = 2 - x
    far = 1 + x
    edge = y == 3 * x
    inner = y != 3 * x
    hands = y != 3 - 3 * x
    place = (2 * z + 1 + x) % EDGES

    def scoped(name):
        return jax.named_scope(name)

    def loads(pair):
        return [
            local(ref.at[:, :, :, pair * 128 : pair * 128 + 128], kv.at[pair, which, 0], load_sem.at[pair, which])
            for which, ref in enumerate((k_ref, v_ref))
        ]

    for pair in range(PAIRS):
        for copy in loads(pair):
            copy.start()

    barrier = pltpu.get_barrier_semaphore()

    def hello(device):
        pl.semaphore_signal(barrier, inc=1, device_id={"seq": device}, device_id_type=MESH)

    with scoped("barrier"):
        peers(me, 1, SEQ, hello)
        pl.semaphore_wait(barrier, SEQ - 1)

    def keep_own(pair):
        return local(kv.at[pair, x, 0, z, y], spread[pair].at[me], own_sem.at[pair])

    def keep(pair):
        for copy in loads(pair):
            copy.wait()
        keep_own(pair).start()

        def send(d):
            dz, dy, dx = split(d)
            remote(kv.at[pair, dx, 0, dz, dy], spread[pair].at[me], p1_send.at[pair], p1_recv.at[pair], d).start()

        peers(me, 1, SEQ, send)

    def kept(pair):
        keep_own(pair).wait()
        drain(spread[pair].at[pl.ds(0, SEQ - 1)], p1_recv.at[pair])

    def to_twin(pair):
        return remote(kv.at[pair, :, 0], kv.at[pair, :, 3 - near], na_send.at[pair], na_recv.at[pair], twin)

    def to_next(pair):
        return remote(kv.at[pair, :, near], kv.at[pair, :, 3 - near], nf_send.at[pair], nf_recv.at[pair], ahead)

    def hand_on(pair):
        to_twin(pair).wait_recv()

        @pl.when(hands)
        def _():
            to_next(pair).start()

    def edge_own(pair):
        mate = edge_block(place)
        return local(spread[pair].at[mate], kv.at[pair, x, far, z, y], own_sem.at[15 + pair])

    def edges(pair):
        @pl.loop(0, EDGES)
        def _(e):
            d = edge_device(e)

            @pl.when(d != me)
            def _():
                remote(
                    spread[pair].at[edge_block(e)], kv.at[pair, x, 2 - e % 2, z, y], pc_send.at[pair], pc_recv.at[pair], d
                ).start()

        @pl.when(edge)
        def _():
            edge_own(pair).start()

    def global_own(pair):
        return local(gsel.at[pair], kv.at[pair, x, 6:8, z, y], own_sem.at[3 + pair])

    def global_z(pair):
        for g in range(2):
            gsel[pair, g] = spread[pair][shared_ids[g]]
        global_own(pair).start()

        @pl.loop(1, NZ)
        def _(k):
            d = ((z + k) % NZ) * 8 + y * 2 + x
            remote(gsel.at[pair], kv.at[pair, x, 6:8, z, y], gz_send.at[pair], gz_recv.at[pair], d).start()

    def across(pair):
        return remote(
            kv.at[pair, x, 6:8, :, y], kv.at[pair, x, 6:8, :, y], gx_send.at[pair], gx_recv.at[pair], twin
        )

    def global_x(pair):
        global_own(pair).wait()
        drain(kv.at[pair, x, 6:8, 0 : NZ - 1, y], gz_recv.at[pair])
        across(pair).start()

    def global_y(pair):
        across(pair).wait_recv()

        @pl.loop(1, NY)
        def _(k):
            d = z * 8 + ((y + k) % NY) * 2 + x
            remote(kv.at[pair, :, 6:8, :, y], kv.at[pair, :, 6:8, :, y], gy_send.at[pair], gy_recv.at[pair], d).start()

    def pick(pair):
        @pl.loop(0, SEQ)
        def _(d):
            for r in range(3):
                picked[pair, d, r] = spread[pair][table[r, d]]

    def route_own(pair):
        return local(picked.at[pair, me], kv.at[pair, x, 3:6, z, y], own_sem.at[6 + pair])

    def routes(pair):
        route_own(pair).start()

        def send(d):
            remote(picked.at[pair, d], kv.at[pair, x, 3:6, z, y], p2_send.at[pair], p2_recv.at[pair], d).start()

        peers(me, 1, SEQ, send)

    def arrive(pair):
        with scoped("arrive_nb%d" % pair):
            @pl.when(inner)
            def _():
                to_next(pair).wait_recv()

            @pl.when(edge)
            def _():
                edge_own(pair).wait()
                drain(spread[pair].at[pl.ds(0, SEQ - 1)], pc_recv.at[pair])
        with scoped("arrive_p2_%d" % pair):
            route_own(pair).wait()
            drain(picked.at[pair, pl.ds(0, SEQ - 1)], p2_recv.at[pair])
        with scoped("arrive_g%d" % pair):
            drain(kv.at[pair, :, 6:8, :, 0 : NY - 1], gy_recv.at[pair])

    def back_far(pair):
        return remote(dkv.at[pair, :, far], far_in.at[pair], bf_send.at[pair], bf_recv.at[pair], behind)

    def back_near(pair):
        return remote(near_out.at[pair], near_in.at[pair], bn_send.at[pair], bn_recv.at[pair], twin)

    def back_own(pair):
        return local(dkv.at[pair, x, 3:6, z, y], coming[pair].at[me], own_sem.at[9 + pair])

    def ret_own(pair):
        return local(ret.at[pair, me], retin.at[pair, x, z, y], own_sem.at[12 + pair])

    def edge_back_own(pair):
        return local(dkv.at[pair, x, far, z, y], extra[pair].at[place], own_sem.at[18 + pair])

    def stage0(pair):
        for k in range(1, NY):
            to = (y + k) % NY
            remote(
                dkv.at[pair, :, 6:8, :, to], rsy.at[pair, k - 1], ry_send.at[pair, k - 1], ry_recv.at[pair, k - 1],
                z * 8 + to * 2 + x,
            ).start()
        @pl.when(inner)
        def _():
            back_far(pair).start()

        @pl.when(edge)
        def _():
            edge_back_own(pair).start()

            def send_edge(d):
                dz, dy, dx = split(d)
                remote(dkv.at[pair, dx, far, dz, dy], extra[pair].at[place], bc_send.at[pair], bc_recv.at[pair], d).start()

            peers(me, 1, SEQ, send_edge)

        back_own(pair).start()

        def send(d):
            dz, dy, dx = split(d)
            remote(dkv.at[pair, dx, 3:6, dz, dy], coming[pair].at[me], b1_send.at[pair], b1_recv.at[pair], d).start()

        peers(me, 1, SEQ, send)

    def back_x(pair):
        return remote(ysum.at[pair, 1 - x], rsx.at[pair], rx_send.at[pair], rx_recv.at[pair], twin)

    def stage1(pair):
        for k in range(1, NY):
            drain(rsy.at[pair, k - 1], ry_recv.at[pair, k - 1])
        for which in range(2):
            total = dkv[pair, which, 6:8, :, y].astype(F32)
            for k in range(NY - 1):
                total = total + rsy[pair, k, which].astype(F32)
            ysum[pair, which] = total.astype(BF)
        back_x(pair).start()

    def relay(pair):
        @pl.when(hands)
        def _():
            back_far(pair).wait_recv()
            for which in range(2):
                total = dkv[pair, which, near].astype(F32) + far_in[pair, which].astype(F32)
                near_out[pair, which] = total.astype(BF)

        @pl.when(y == 3 - 3 * x)
        def _():
            for which in range(2):
                near_out[pair, which] = dkv[pair, which, near]

        back_near(pair).start()

    def stage2(pair):
        back_x(pair).wait_recv()
        xsum[pair] = (ysum[pair, x].astype(F32) + rsx[pair].astype(F32)).astype(BF)
        for k in range(1, NZ):
            to = (z + k) % NZ
            remote(
                xsum.at[pair, :, to], rsz.at[pair, k - 1], rz_send.at[pair, k - 1], rz_recv.at[pair, k - 1],
                to * 8 + y * 2 + x,
            ).start()

    def stage3(pair):
        for k in range(1, NZ):
            drain(rsz.at[pair, k - 1], rz_recv.at[pair, k - 1])
        shared = xsum[pair, :, z].astype(F32)
        for k in range(NZ - 1):
            shared = shared + rsz[pair, k].astype(F32)
        back_own(pair).wait()
        drain(coming[pair].at[pl.ds(0, SEQ - 1)], b1_recv.at[pair])

        @pl.when(edge)
        def _():
            edge_back_own(pair).wait()
            drain(extra[pair].at[pl.ds(0, EDGES - 1)], bc_recv.at[pair])

        @pl.when(inner)
        def _():
            drain(extra[pair], bc_recv.at[pair])

        def total_of(c):
            total = sum((shared_ids[g] == c).astype(F32) * shared[g] for g in range(2))
            for r in range(3):
                total = total + coming[pair][inverse[r, c], r].astype(F32)
            return total

        @pl.loop(0, SEQ)
        def _(c):
            ret[pair, c] = total_of(c).astype(BF)

        @pl.loop(0, EDGES)
        def _(e):
            c = edge_block(e)
            ret[pair, c] = (total_of(c) + extra[pair][e].astype(F32)).astype(BF)

        ret_own(pair).start()

        def send(d):
            remote(ret.at[pair, d], retin.at[pair, x, z, y], b2_send.at[pair], b2_recv.at[pair], d).start()

        peers(me, 1, SEQ, send)

    def stage4(pair):
        back_near(pair).wait_recv()
        ret_own(pair).wait()
        drain(ret.at[pair, pl.ds(0, SEQ - 1)], b2_recv.at[pair])
        for which, ref in enumerate((gk_ref, gv_ref)):
            total = dkv[pair, which, 0].astype(F32) + retin[pair, which].astype(F32) + near_in[pair, which].astype(F32)
            ref[:, pair * 128 : pair * 128 + 128] = rows(total.astype(BF))

    def finish(pair):
        cols = slice(pair * 128, pair * 128 + 128)
        o_ref[:, cols] = ot[...].T.astype(BF)
        dq_ref[:, cols] = dqt[...].T.astype(BF)

    def run(work):
        for stage, pair in work:
            with scoped("%s_%d" % (stage.__name__, pair)):
                stage(pair)

    def compute(pair, *work):
        arrive(pair)
        prepare(pair, kv, q_ref, do_ref, kt, vt, qt, qm)
        for h in range(2):
            ticks = [functools.partial(run, work[3 * h + i]) for i in range(3)]
            head(pair, h, ticks, kv, dkv, do_ref, ot, dqt, s_buf, p_buf, kt, vt, qt, qm)
            ticks[2]()
        with scoped("stage0_%d" % pair):
            stage0(pair)
        finish(pair)

    def to_twin_start(pair):
        to_twin(pair).start()

    run([(keep, 0), (keep, 1), (keep, 2), (to_twin_start, 0), (to_twin_start, 1), (to_twin_start, 2)])
    run([(kept, 0), (global_z, 0), (kept, 1), (global_z, 1), (kept, 2), (global_z, 2), (pick, 0), (edges, 0), (routes, 0)])
    run([(hand_on, 0), (global_x, 0), (global_x, 1), (global_x, 2), (pick, 1), (pick, 2), (hand_on, 1)])
    run([(global_y, 0), (edges, 1), (routes, 1), (hand_on, 2), (global_y, 1), (edges, 2), (routes, 2), (global_y, 2)])
    compute(0, [], [], [], [], [], [])
    compute(1, [], [], [], [], [(stage1, 0)], [(stage2, 0)])
    compute(2, [(relay, 0)], [], [], [(stage3, 0)], [(stage1, 1)], [(stage2, 1)])
    run([(relay, 1), (stage1, 2), (stage3, 1), (stage2, 2), (stage4, 0), (relay, 2), (stage3, 2), (stage4, 1), (stage4, 2)])

    for pair in range(PAIRS):
        drain(spread[pair].at[pl.ds(0, SEQ - 1)], p1_send.at[pair])
        drain(kv.at[pair, x, 6:8, 0 : NZ - 1, y], gz_send.at[pair])
        for copy in (to_twin(pair), across(pair), back_near(pair), back_x(pair)):
            copy.wait_send()

        @pl.when(hands)
        def _():
            to_next(pair).wait_send()

        @pl.when(inner)
        def _():
            back_far(pair).wait_send()
            drain(extra[pair], pc_send.at[pair])

        @pl.when(edge)
        def _():
            drain(extra[pair].at[pl.ds(0, EDGES - 1)], pc_send.at[pair])
            drain(spread[pair].at[pl.ds(0, SEQ - 1)], bc_send.at[pair])

        drain(picked.at[pair, pl.ds(0, SEQ - 1)], p2_send.at[pair])
        drain(kv.at[pair, :, 6:8, :, 0 : NY - 1], gy_send.at[pair])
        drain(coming[pair].at[pl.ds(0, SEQ - 1)], b1_send.at[pair])
        for k in range(NY - 1):
            drain(rsy.at[pair, k], ry_send.at[pair, k])
        for k in range(NZ - 1):
            drain(rsz.at[pair, k], rz_send.at[pair, k])
        drain(ret.at[pair, pl.ds(0, SEQ - 1)], b2_send.at[pair])


def step(queries, key_states, value_states, grad_output, partners, global_blocks):
    ids = jnp.arange(SEQ, dtype=jnp.int32)
    inverse = jnp.sum(jnp.where(partners[:, :, None] == ids[None, None, :], ids[None, :, None], 0), axis=1)
    vmem = pl.BlockSpec(memory_space=pltpu.VMEM)
    smem = pl.BlockSpec(memory_space=pltpu.SMEM)
    anywhere = pl.BlockSpec(memory_space=pl.ANY)
    scratch = [
        pltpu.VMEM((PAIRS, 2, 8, NZ, NY, 16, 128), BF),
        pltpu.VMEM((PAIRS, 2, 8, NZ, NY, 16, 128), BF),
        pltpu.VMEM((SEQ, 16, 128), BF),
        pltpu.VMEM((SEQ, 16, 128), BF),
        pltpu.VMEM((SEQ, 16, 128), BF),
        pltpu.VMEM((PAIRS, SEQ, 3, 16, 128), BF),
        pltpu.VMEM((PAIRS, 2, 16, 128), BF),
        pltpu.VMEM((SEQ, 3, 16, 128), BF),
        pltpu.VMEM((SEQ, 3, 16, 128), BF),
        pltpu.VMEM((SEQ, 3, 16, 128), BF),
        pltpu.VMEM((EDGES, 16, 128), BF),
        pltpu.VMEM((EDGES, 16, 128), BF),
        pltpu.VMEM((EDGES, 16, 128), BF),
        pltpu.VMEM((PAIRS, 2, NZ, NY, 16, 128), BF),
        pltpu.VMEM((PAIRS, 2, NZ, NY, 16, 128), BF),
        pltpu.VMEM((PAIRS, 2, NZ, NY, 16, 128), BF),
        pltpu.VMEM((PAIRS, NY - 1, 2, 2, NZ, 16, 128), BF),
        pltpu.VMEM((PAIRS, 2, 2, NZ, 16, 128), BF),
        pltpu.VMEM((PAIRS, 2, NZ, 16, 128), BF),
        pltpu.VMEM((PAIRS, 2, NZ, 16, 128), BF),
        pltpu.VMEM((PAIRS, NZ - 1, 2, 16, 128), BF),
        pltpu.VMEM((PAIRS, SEQ, 16, 128), BF),
        pltpu.VMEM((PAIRS, 2, NZ, NY, 16, 128), BF),
        pltpu.VMEM((8, BLOCK, BLOCK), F32),
        pltpu.VMEM((8, BLOCK, BLOCK), BF),
        pltpu.VMEM((8, 128, BLOCK), BF),
        pltpu.VMEM((2, 8, 80, BLOCK), BF),
        pltpu.VMEM((2, 128, BLOCK), BF),
        pltpu.VMEM((2, BLOCK, 128), BF),
        pltpu.VMEM((128, BLOCK), F32),
        pltpu.VMEM((128, BLOCK), F32),
    ]
    dma = pltpu.SemaphoreType.DMA
    sems = [dma((PAIRS, 2)), dma((7 * PAIRS,))]
    sems += [dma((PAIRS,)) for _ in range(24)]
    sems += [dma((PAIRS, NY - 1)) for _ in range(2)] + [dma((PAIRS,)) for _ in range(2)]
    sems += [dma((PAIRS, NZ - 1)) for _ in range(2)] + [dma((PAIRS,)) for _ in range(2)]
    grid_rows = (NZ, NY, 16, PAIRS * 128)
    return pl.pallas_call(
        kernel,
        out_shape=tuple(jax.ShapeDtypeStruct((BLOCK, PAIRS * 128), BF) for _ in range(4)),
        in_specs=[smem, smem, smem, vmem, vmem, anywhere, anywhere],
        out_specs=(vmem,) * 4,
        scratch_shapes=scratch + sems,
        compiler_params=pltpu.CompilerParams(
            collective_id=0, has_side_effects=True, vmem_limit_bytes=60 * 1024 * 1024
        ),
    )(partners, inverse, global_blocks, queries, grad_output, key_states.reshape(grid_rows), value_states.reshape(grid_rows))


def solution(mesh):
    spec = P(("batch", "seq"), None)
    return jax.shard_map(
        step,
        mesh=mesh,
        in_specs=(spec, spec, spec, spec, P("batch", None), P("batch")),
        out_specs=(spec,) * 4,
        check_vma=False,
    )
```

time: 229 us -> 201 us (0.88)
  Pallas kernels: 220 us -> 191 us
    pallas_call x1, Pallas kernels: 220 us -> 191 us  [step(): pl.pallas_call(kernel, out_shape=tuple((jax.ShapeDtypeStruct((BLOCK, PAIR...]
    unnamed x14 -> x12, local copies, waits for them, and re-layouts: 5.51 us -> 5.53 us
where the time goes in v2:
time: 201 us; the launch traced here: 198 us
  Pallas kernels  191 us (95%)
  local copies, waits for them, and re-layouts  5.53 us (3%)
    pallas_call x1, Pallas kernels, step(): pl.pallas_call(kernel, out_shape=tuple((jax.ShapeDtypeStruct((BLOCK, PAIR...  191 us
    unnamed x12, local copies, waits for them, and re-layouts  5.53 us

profile of v2, /device:TPU:28, one launch (start us, length us, event | category | flops | bytes accessed | tf_op | source)
XLA Modules:
  0.0 198.4 jit_solution(9586222534883114852)
XLA Ops:
  0.6 0.0 copy-start.3
  0.6 0.7 copy-done.3
  1.3 0.7 select_reduce_fusion.inverse
  2.0 191.5 %shard_map.93 = (bf16[512,384]{1,0:T(8,128)(2,1)}, bf16[512,384]{1,0:T(8,128)(2,1)}, bf16[512,384]{1,0:T(8,128)(2,1)}, bf16[512,384]{1,0:T(8,128)(2,1)}) custom-call(s32[3,64]{1,0:T(4,128)} %table.1, s32[3,64]{1,0:T(4,128)} %select_reduce_fusion.inverse, s32[2]{0:T(128)} %shared_ids.1, bf16[512,384]{1,0:T(8,128)(2,1)} %q_ref.1, bf16[512,384]{1,0:T(8,128)(2,1)} %do_ref.1, ...), custom_call_target="tpu_custom_call" | custom-call | tf_op jit(solution)/shard_map/pallas_call | solution.py:532
  193.5 0.0 copy-start.2
  193.5 1.8 copy.14
  195.3 0.0 copy-done.2
  195.3 0.0 copy-start.1
  195.3 0.7 copy.15
  196.1 0.4 copy-done.1
  196.5 0.0 copy-start
  196.5 0.7 copy.16
  197.2 0.4 copy-done
  197.6 0.7 copy.17
Async XLA Ops:
  0.6 0.7 copy-start.3
  193.5 1.8 copy-start.2
  195.3 1.1 copy-start.1
  196.5 1.1 copy-start

commit v3 on v2

--- a/solution.py
+++ b/solution.py
@@ -18,6 +18,7 @@
 SEQ = 64
 NZ, NY = 8, 4
 EDGES = 16
+PARTS = ((0, 3), (3, 6), (6, 8))
 
 
 def split(device):
@@ -60,7 +61,7 @@
     return block.reshape(NZ, NY, 16, 128)
 
 
-def prepare(pair, kv, q_ref, do_ref, kt, vt, qt, qm):
+def prepare(pair, q_ref, qt, qm):
     cols = slice(pair * 128, pair * 128 + 128)
     qs = q_ref[:, cols] * jnp.asarray(0.125, BF)
     lane = lax.broadcasted_iota(jnp.int32, (BLOCK, 128), 1)
@@ -70,7 +71,9 @@
         qm[h] = jnp.where((lane >= 64) == (h == 1), qs, jnp.zeros_like(qs))
         qt[h] = jnp.where((row >= 64) == (h == 1), qst, jnp.zeros_like(qst))
 
-    @pl.loop(0, 8)
+
+def turn(pair, first, last, kv, kt, vt):
+    @pl.loop(first, last)
     def _(j):
         kt[j] = rows(kv[pair, 0, j]).T
         t = rows(kv[pair, 1, j]).T
@@ -79,7 +82,7 @@
             vt[h, j, 64:80] = jnp.ones((16, BLOCK), BF)
 
 
-def head(pair, h, ticks, kv, dkv, do_ref, ot, dqt, s_buf, p_buf, kt, vt, qt, qm):
+def head(pair, h, gates, ticks, sends, kv, dkv, do_ref, ot, dqt, s_buf, p_buf, kt, vt, qt, qm):
     do_t = do_ref[:, pair * 128 : pair * 128 + 128].astype(F32).T
     qth = qt[h]
 
@@ -88,7 +91,10 @@
         s_buf[j] = s
         return jnp.maximum(peak, jnp.max(s.reshape(BLOCK // 8, 8, BLOCK), axis=0))
 
-    peak = lax.fori_loop(0, 8, scores, jnp.full((8, BLOCK), -jnp.inf, F32))
+    peak = jnp.full((8, BLOCK), -jnp.inf, F32)
+    for gate, (first, last) in zip(gates, PARTS):
+        gate(first, last)
+        peak = lax.fori_loop(first, last, scores, peak)
     peak = jnp.max(peak, axis=0, keepdims=True) * LOG2E
     ticks[0]()
 
@@ -123,7 +129,10 @@
             dkv[pair, 1, j] = dkv[pair, 1, j] + tiles(dv)
         return acc + jnp.dot(kt[j, 64 * h : 64 * h + 64], ds, preferred_element_type=F32)
 
-    dq = lax.fori_loop(0, 8, backward, jnp.zeros((64, BLOCK), F32))
+    dq = jnp.zeros((64, BLOCK), F32)
+    for send, (first, last) in zip(sends, PARTS[::-1]):
+        dq = lax.fori_loop(first, last, backward, dq)
+        send()
     dqt[64 * h : 64 * h + 64] = dq * 0.125
 
 
@@ -235,10 +244,13 @@
             gsel[pair, g] = spread[pair][shared_ids[g]]
         global_own(pair).start()
 
-        @pl.loop(1, NZ)
+        @pl.loop(1, 2 * NZ if pair == 0 else NZ)
         def _(k):
-            d = ((z + k) % NZ) * 8 + y * 2 + x
+            d = plane(k) if pair == 0 else ((z + k) % NZ) * 8 + y * 2 + x
             remote(gsel.at[pair], kv.at[pair, x, 6:8, z, y], gz_send.at[pair], gz_recv.at[pair], d).start()
+
+    def plane(k):
+        return ((z + k // 2) % NZ) * 8 + y * 2 + (x + k) % 2
 
     def across(pair):
         return remote(
@@ -251,7 +263,11 @@
         across(pair).start()
 
     def global_y(pair):
-        across(pair).wait_recv()
+        if pair == 0:
+            global_own(pair).wait()
+            drain(picked.at[pair, pl.ds(0, 10)], gz_recv.at[pair])
+        else:
+            across(pair).wait_recv()
 
         @pl.loop(1, NY)
         def _(k):
@@ -275,21 +291,22 @@
 
         peers(me, 1, SEQ, send)
 
-    def arrive(pair):
-        with scoped("arrive_nb%d" % pair):
-            @pl.when(inner)
-            def _():
-                to_next(pair).wait_recv()
-
-            @pl.when(edge)
-            def _():
-                edge_own(pair).wait()
-                drain(spread[pair].at[pl.ds(0, SEQ - 1)], pc_recv.at[pair])
-        with scoped("arrive_p2_%d" % pair):
-            route_own(pair).wait()
-            drain(picked.at[pair, pl.ds(0, SEQ - 1)], p2_recv.at[pair])
-        with scoped("arrive_g%d" % pair):
-            drain(kv.at[pair, :, 6:8, :, 0 : NY - 1], gy_recv.at[pair])
+    def arrive_near(pair):
+        @pl.when(inner)
+        def _():
+            to_next(pair).wait_recv()
+
+        @pl.when(edge)
+        def _():
+            edge_own(pair).wait()
+            drain(spread[pair].at[pl.ds(0, SEQ - 1)], pc_recv.at[pair])
+
+    def arrive_routes(pair):
+        route_own(pair).wait()
+        drain(picked.at[pair, pl.ds(0, SEQ - 1)], p2_recv.at[pair])
+
+    def arrive_global(pair):
+        drain(kv.at[pair, :, 6:8, :, 0 : NY - 1], gy_recv.at[pair])
 
     def back_far(pair):
         return remote(dkv.at[pair, :, far], far_in.at[pair], bf_send.at[pair], bf_recv.at[pair], behind)
@@ -306,13 +323,24 @@
     def edge_back_own(pair):
         return local(dkv.at[pair, x, far, z, y], extra[pair].at[place], own_sem.at[18 + pair])
 
-    def stage0(pair):
+    def back_global(pair):
         for k in range(1, NY):
             to = (y + k) % NY
             remote(
                 dkv.at[pair, :, 6:8, :, to], rsy.at[pair, k - 1], ry_send.at[pair, k - 1], ry_recv.at[pair, k - 1],
                 z * 8 + to * 2 + x,
             ).start()
+
+    def back_routes(pair):
+        back_own(pair).start()
+
+        def send(d):
+            dz, dy, dx = split(d)
+            remote(dkv.at[pair, dx, 3:6, dz, dy], coming[pair].at[me], b1_send.at[pair], b1_recv.at[pair], d).start()
+
+        peers(me, 1, SEQ, send)
+
+    def back_beyond(pair):
         @pl.when(inner)
         def _():
             back_far(pair).start()
@@ -326,14 +354,6 @@
                 remote(dkv.at[pair, dx, far, dz, dy], extra[pair].at[place], bc_send.at[pair], bc_recv.at[pair], d).start()
 
             peers(me, 1, SEQ, send_edge)
-
-        back_own(pair).start()
-
-        def send(d):
-            dz, dy, dx = split(d)
-            remote(dkv.at[pair, dx, 3:6, dz, dy], coming[pair].at[me], b1_send.at[pair], b1_recv.at[pair], d).start()
-
-        peers(me, 1, SEQ, send)
 
     def back_x(pair):
         return remote(ysum.at[pair, 1 - x], rsx.at[pair], rx_send.at[pair], rx_recv.at[pair], twin)
@@ -432,14 +452,28 @@
                 stage(pair)
 
     def compute(pair, *work):
-        arrive(pair)
-        prepare(pair, kv, q_ref, do_ref, kt, vt, qt, qm)
+        prepare(pair, q_ref, qt, qm)
+
+        def gated(arrive):
+            def gate(first, last):
+                run([(arrive, pair)])
+                turn(pair, first, last, kv, kt, vt)
+
+            return gate
+
+        def nothing(*_):
+            return None
+
         for h in range(2):
             ticks = [functools.partial(run, work[3 * h + i]) for i in range(3)]
-            head(pair, h, ticks, kv, dkv, do_ref, ot, dqt, s_buf, p_buf, kt, vt, qt, qm)
+            if h == 0:
+                gates = [gated(arrive) for arrive in (arrive_near, arrive_routes, arrive_global)]
+                sends = [nothing] * 3
+            else:
+                gates = [nothing] * 3
+                sends = [functools.partial(run, [(stage, pair)]) for stage in (back_global, back_routes, back_beyond)]
+            head(pair, h, gates, ticks, sends, kv, dkv, do_ref, ot, dqt, s_buf, p_buf, kt, vt, qt, qm)
             ticks[2]()
-        with scoped("stage0_%d" % pair):
-            stage0(pair)
         finish(pair)
 
     def to_twin_start(pair):
@@ -447,17 +481,21 @@
 
     run([(keep, 0), (keep, 1), (keep, 2), (to_twin_start, 0), (to_twin_start, 1), (to_twin_start, 2)])
     run([(kept, 0), (global_z, 0), (kept, 1), (global_z, 1), (kept, 2), (global_z, 2), (pick, 0), (edges, 0), (routes, 0)])
-    run([(hand_on, 0), (global_x, 0), (global_x, 1), (global_x, 2), (pick, 1), (pick, 2), (hand_on, 1)])
-    run([(global_y, 0), (edges, 1), (routes, 1), (hand_on, 2), (global_y, 1), (edges, 2), (routes, 2), (global_y, 2)])
-    compute(0, [], [], [], [], [], [])
-    compute(1, [], [], [], [], [(stage1, 0)], [(stage2, 0)])
-    compute(2, [(relay, 0)], [], [], [(stage3, 0)], [(stage1, 1)], [(stage2, 1)])
-    run([(relay, 1), (stage1, 2), (stage3, 1), (stage2, 2), (stage4, 0), (relay, 2), (stage3, 2), (stage4, 1), (stage4, 2)])
+    run([(hand_on, 0), (global_y, 0), (global_x, 1), (global_x, 2), (pick, 1), (pick, 2), (hand_on, 1)])
+    run([(global_y, 1), (edges, 1), (routes, 1), (hand_on, 2)])
+    compute(0, [(edges, 2), (routes, 2)], [(global_y, 2)], [], [], [], [])
+    compute(1, [], [], [], [], [], [])
+    compute(2, [(relay, 0)], [(stage1, 0)], [], [(stage2, 0), (stage1, 1)], [(relay, 1)], [(stage2, 1)])
+    run([(stage3, 0), (stage1, 2), (stage3, 1), (stage2, 2), (relay, 2), (stage3, 2), (stage4, 0), (stage4, 1), (stage4, 2)])
 
     for pair in range(PAIRS):
         drain(spread[pair].at[pl.ds(0, SEQ - 1)], p1_send.at[pair])
-        drain(kv.at[pair, x, 6:8, 0 : NZ - 1, y], gz_send.at[pair])
-        for copy in (to_twin(pair), across(pair), back_near(pair), back_x(pair)):
+        if pair == 0:
+            drain(picked.at[pair, pl.ds(0, 10)], gz_send.at[pair])
+        else:
+            drain(kv.at[pair, x, 6:8, 0 : NZ - 1, y], gz_send.at[pair])
+            across(pair).wait_send()
+        for copy in (to_twin(pair), back_near(pair)):
             copy.wait_send()
 
         @pl.when(hands)
@@ -479,9 +517,15 @@
         drain(coming[pair].at[pl.ds(0, SEQ - 1)], b1_send.at[pair])
         for k in range(NY - 1):
             drain(rsy.at[pair, k], ry_send.at[pair, k])
+        back_x(pair).wait_send()
         for k in range(NZ - 1):
             drain(rsz.at[pair, k], rz_send.at[pair, k])
         drain(ret.at[pair, pl.ds(0, SEQ - 1)], b2_send.at[pair])
+
+
+def put(*refs):
+    for src, dst in zip(refs[:4], refs[4:]):
+        dst[...] = src[...]
 
 
 def step(queries, key_states, value_states, grad_output, partners, global_blocks):
@@ -529,9 +573,10 @@
     sems += [dma((PAIRS, NY - 1)) for _ in range(2)] + [dma((PAIRS,)) for _ in range(2)]
     sems += [dma((PAIRS, NZ - 1)) for _ in range(2)] + [dma((PAIRS,)) for _ in range(2)]
     grid_rows = (NZ, NY, 16, PAIRS * 128)
-    return pl.pallas_call(
+    shapes = tuple(jax.ShapeDtypeStruct((BLOCK, PAIRS * 128), BF) for _ in range(4))
+    results = pl.pallas_call(
         kernel,
-        out_shape=tuple(jax.ShapeDtypeStruct((BLOCK, PAIRS * 128), BF) for _ in range(4)),
+        out_shape=shapes,
         in_specs=[smem, smem, smem, vmem, vmem, anywhere, anywhere],
         out_specs=(vmem,) * 4,
         scratch_shapes=scratch + sems,
@@ -539,6 +584,7 @@
             collective_id=0, has_side_effects=True, vmem_limit_bytes=60 * 1024 * 1024
         ),
     )(partners, inverse, global_blocks, queries, grad_output, key_states.reshape(grid_rows), value_states.reshape(grid_rows))
+    return pl.pallas_call(put, out_shape=shapes, in_specs=[vmem] * 4, out_specs=(vmem,) * 4)(*results)
 
 
 def solution(mesh):

time: 201 us -> 194 us (0.965)
  local copies, waits for them, and re-layouts: 5.53 us -> 0.68 us
    unnamed x12 -> x2, local copies, waits for them, and re-layouts: 5.53 us -> 0.68 us
    pallas_call x1 -> x2, Pallas kernels: 191 us -> 191 us  [the longest x1 189 us: step(): pl.pallas_call(kernel, out_shape=shapes, in_specs=[smem, smem, smem, vmem...]
where the time goes in v3:
time: 194 us; the launch traced here: 193 us
  Pallas kernels  191 us (98%)
    pallas_call x1, Pallas kernels, step(): pl.pallas_call(kernel, out_shape=shapes, in_specs=[smem, smem, smem, vmem...  189 us

profile of v3, /device:TPU:28, one launch (start us, length us, event | category | flops | bytes accessed | tf_op | source)
XLA Modules:
  0.0 193.3 jit_solution(5440611079792034794)
XLA Ops:
  0.6 0.0 copy-start
  0.6 0.7 copy-done
  1.3 0.7 select_reduce_fusion.inverse
  2.0 188.8 %shard_map.93 = (bf16[512,384]{1,0:T(8,128)(2,1)}, bf16[512,384]{1,0:T(8,128)(2,1)}, bf16[512,384]{1,0:T(8,128)(2,1)}, bf16[512,384]{1,0:T(8,128)(2,1)}) custom-call(s32[3,64]{1,0:T(4,128)} %table.1, s32[3,64]{1,0:T(4,128)} %select_reduce_fusion.inverse, s32[2]{0:T(128)} %shared_ids.1, bf16[512,384]{1,0:T(8,128)(2,1)} %q_ref.1, bf16[512,384]{1,0:T(8,128)(2,1)} %do_ref.1, ...), custom_call_target="tpu_custom_call" | custom-call | tf_op jit(solution)/shard_map/pallas_call | solution.py:577
  190.8 2.5 %shard_map.94 = (bf16[512,384]{1,0:T(8,128)(2,1)}, bf16[512,384]{1,0:T(8,128)(2,1)}, bf16[512,384]{1,0:T(8,128)(2,1)}, bf16[512,384]{1,0:T(8,128)(2,1)}) custom-call(bf16[512,384]{1,0:T(8,128)(2,1)} %get-tuple-element.8.refs_0_, bf16[512,384]{1,0:T(8,128)(2,1)} %get-tuple-element.9.refs_1_, bf16[512,384]{1,0:T(8,128)(2,1)} %get-tuple-element.10.refs_2_, ...), custom_call_target="tpu_custom_call" | custom-call | tf_op jit(solution)/shard_map/pallas_call | solution.py:587
Async XLA Ops:
  0.6 0.7 copy-start

commit v4 on v3

--- a/solution.py
+++ b/solution.py
@@ -481,8 +481,8 @@
 
     run([(keep, 0), (keep, 1), (keep, 2), (to_twin_start, 0), (to_twin_start, 1), (to_twin_start, 2)])
     run([(kept, 0), (global_z, 0), (kept, 1), (global_z, 1), (kept, 2), (global_z, 2), (pick, 0), (edges, 0), (routes, 0)])
-    run([(hand_on, 0), (global_y, 0), (global_x, 1), (global_x, 2), (pick, 1), (pick, 2), (hand_on, 1)])
-    run([(global_y, 1), (edges, 1), (routes, 1), (hand_on, 2)])
+    run([(hand_on, 0), (pick, 1), (edges, 1), (global_y, 0), (routes, 1), (global_x, 1), (global_x, 2)])
+    run([(hand_on, 1), (hand_on, 2), (pick, 2), (global_y, 1)])
     compute(0, [(edges, 2), (routes, 2)], [(global_y, 2)], [], [], [], [])
     compute(1, [], [], [], [], [], [])
     compute(2, [(relay, 0)], [(stage1, 0)], [], [(stage2, 0), (stage1, 1)], [(relay, 1)], [(stage2, 1)])
@@ -524,8 +524,16 @@
 
 
 def put(*refs):
-    for src, dst in zip(refs[:4], refs[4:]):
-        dst[...] = src[...]
+    buffers, load_sem, store_sem = refs[8:]
+    loads = [local(refs[i], buffers.at[i], load_sem.at[i]) for i in range(4)]
+    stores = [local(buffers.at[i], refs[4 + i], store_sem.at[i]) for i in range(4)]
+    for copy in loads:
+        copy.start()
+    for load, store in zip(loads, stores):
+        load.wait()
+        store.start()
+    for copy in stores:
+        copy.wait()
 
 
 def step(queries, key_states, value_states, grad_output, partners, global_blocks):
@@ -584,7 +592,13 @@
             collective_id=0, has_side_effects=True, vmem_limit_bytes=60 * 1024 * 1024
         ),
     )(partners, inverse, global_blocks, queries, grad_output, key_states.reshape(grid_rows), value_states.reshape(grid_rows))
-    return pl.pallas_call(put, out_shape=shapes, in_specs=[vmem] * 4, out_specs=(vmem,) * 4)(*results)
+    return pl.pallas_call(
+        put,
+        out_shape=shapes,
+        in_specs=[anywhere] * 4,
+        out_specs=(anywhere,) * 4,
+        scratch_shapes=[pltpu.VMEM((4, BLOCK, PAIRS * 128), BF), dma((4,)), dma((4,))],
+    )(*results)
 
 
 def solution(mesh):

time: 194 us -> 201 us (1.036)
  the two profiles are of different devices: /device:TPU:28 before, /device:TPU:6 now
where the time goes in v4:
time: 201 us
  Pallas kernels  198 us (99%)
    pallas_call x1, Pallas kernels, step(): pl.pallas_call(kernel, out_shape=shapes, in_specs=[smem, smem, smem, vmem...  196 us

profile of v4, /device:TPU:6, one launch (start us, length us, event | category | flops | bytes accessed | tf_op | source)
XLA Modules:
  0.0 200.7 jit_solution(17372396439947879128)
XLA Ops:
  0.6 0.0 copy-start
  0.6 0.7 copy-done
  1.3 0.7 select_reduce_fusion.inverse
  2.0 196.3 %shard_map.93 = (bf16[512,384]{1,0:T(8,128)(2,1)}, bf16[512,384]{1,0:T(8,128)(2,1)}, bf16[512,384]{1,0:T(8,128)(2,1)}, bf16[512,384]{1,0:T(8,128)(2,1)}) custom-call(s32[3,64]{1,0:T(4,128)} %table.1, s32[3,64]{1,0:T(4,128)} %select_reduce_fusion.inverse, s32[2]{0:T(128)} %shared_ids.1, bf16[512,384]{1,0:T(8,128)(2,1)} %q_ref.1, bf16[512,384]{1,0:T(8,128)(2,1)} %do_ref.1, ...), custom_call_target="tpu_custom_call" | custom-call | tf_op jit(solution)/shard_map/pallas_call | solution.py:585
  198.3 2.2 %shard_map.94 = (bf16[512,384]{1,0:T(8,128)(2,1)}, bf16[512,384]{1,0:T(8,128)(2,1)}, bf16[512,384]{1,0:T(8,128)(2,1)}, bf16[512,384]{1,0:T(8,128)(2,1)}) custom-call(bf16[512,384]{1,0:T(8,128)(2,1)} %get-tuple-element.8.refs_0_, bf16[512,384]{1,0:T(8,128)(2,1)} %get-tuple-element.9.refs_1_, bf16[512,384]{1,0:T(8,128)(2,1)} %get-tuple-element.10.refs_2_, ...), custom_call_target="tpu_custom_call" | custom-call | tf_op jit(solution)/shard_map/pallas_call | solution.py:595
Async XLA Ops:
  0.6 0.7 copy-start
